TPU v7x, 32 devices: a whole 2x2x4 slice. The times are simulated.
32 devices in a mesh: dp: 4 (over z), row: 4 (over y, core), col: 2 (over x).
Axes of the slice: x: 2, y: 2, z: 4, core: 2. Of those that a mesh axis runs over, the one named last changes fastest.
Arguments:
- block_in: float32 [4, 1024, 1024], P('dp', 'row', 'col'), may hold values from -37 to 37
- out_grad: float32 [4, 1024, 1024], P('dp', 'row', 'col'), may hold values from -6 to 6
- segment_ids: int32 [4, 1024], P('dp'), may hold values from 0 to 2, never falling along the last dimension, each value on 1 to 512 neighbouring positions
- attn_gain: float32 [1024], P('col'), may hold values from 0.5 to 1.5
- w_query: bfloat16 [1024, 1024], P('col', 'row'), may hold values from -0.125 to 0.125
- w_key: bfloat16 [1024, 512], P('col', 'row'), may hold values from -0.125 to 0.125
- w_value: bfloat16 [1024, 512], P('col', 'row'), may hold values from -0.1875 to 0.1875
- query_gain: float32 [64], replicated, may hold values from 0.5 to 5.5
- key_gain: float32 [64], replicated, may hold values from 0.5 to 5.5
- w_out: bfloat16 [1024, 1024], P('row', 'col'), may hold values from -1.5 to 1.5
- ffn_gain: float32 [1024], P('col'), may hold values from 0.5 to 1.5
- w_gate: bfloat16 [1024, 4608], P('col', 'row'), may hold values from -0.1875 to 0.1875
- w_up: bfloat16 [1024, 4608], P('col', 'row'), may hold values from -0.1875 to 0.1875
- w_down: bfloat16 [4608, 1024], P('row', 'col'), may hold values from -0.09375 to 0.09375
Outputs:
- block_out: float32 [4, 1024, 1024], P('dp', 'row', 'col')
- in_grad: float32 [4, 1024, 1024], P('dp', 'row', 'col')
- grad_attn_gain: float32 [1024], P('col')
- grad_query: float32 [1024, 1024], P('col', 'row')
- grad_key: float32 [1024, 512], P('col', 'row')
- grad_value: float32 [1024, 512], P('col', 'row')
- grad_query_gain: float32 [64], replicated
- grad_key_gain: float32 [64], replicated
- grad_out: float32 [1024, 1024], P('row', 'col')
- grad_ffn_gain: float32 [1024], P('col')
- grad_gate: float32 [1024, 4608], P('col', 'row')
- grad_up: float32 [1024, 4608], P('col', 'row')
- grad_down: float32 [4608, 1024], P('row', 'col')
Inputs may be any that keep to these rules, and one draw needn't show every extreme that they name: `segment_ids`: in each sequence the numbers never fall along the positions; each document holds 1 to 512 tokens and some document holds exactly 512.
All inputs are finite; a program needn't handle non-finite values.
Results may differ from a plain program's by a relative error of at most 0.028.
The roundings to bfloat16 on the way count: a program that leaves them out, or rounds other values in their place, can miss the bound.
Values may be sent and summed in bfloat16 or wider, within the bound.
No kernel may reach another device: no remote copies, remote signals or barrier semaphores. Data moves between devices by JAX's collectives and lax.ppermute only.
A program may use at most 128 MiB of HBM per device.

v0:
```python
import jax
import jax.numpy as jnp
from jax import lax
from jax.sharding import PartitionSpec as P

NORM_EPSILON = 1e-05
ROPE_BASE = 1000000.0


def rope_tables(length, head_width):
    half_width = head_width // 2
    exponents = jnp.arange(half_width, dtype=jnp.float32) * (2.0 / head_width)
    frequency = ROPE_BASE ** (-exponents)
    angles = jnp.arange(length, dtype=jnp.float32)[:, None] * frequency[None, :]
    return (jnp.cos(angles), jnp.sin(angles))


def rotate(vectors, cosine, sine, direction):
    half_width = vectors.shape[-1] // 2
    first_half = vectors[..., :half_width]
    second_half = vectors[..., half_width:]
    cos_rows = cosine[:, None, :]
    sin_rows = sine[:, None, :] * direction
    return jnp.concatenate(
        [
            first_half * cos_rows - second_half * sin_rows,
            second_half * cos_rows + first_half * sin_rows,
        ],
        axis=-1,
    )


def col_total(values):
    return lax.psum(values, "col")


def all_rows(local_part):
    return lax.all_gather(local_part, "row", axis=0, tiled=True)


def head_gather(local_part):
    return lax.all_gather(local_part, "col", axis=1, tiled=True)


def back_sums(partial_terms):
    return lax.psum_scatter(partial_terms, "col", scatter_dimension=1, tiled=True)


def contract_rows(left, right):
    return lax.dot_general(
        left, right, (((0,), (0,)), ((), ())), preferred_element_type=jnp.float32
    )


def times_transposed(left, right):
    return lax.dot_general(
        left, right, (((1,), (1,)), ((), ())), preferred_element_type=jnp.float32
    )


def scatter_rows(left, right, transposed):

    def term():
        if transposed:
            return times_transposed(left, right)
        return jnp.dot(left, right, preferred_element_type=jnp.float32)

    return lax.psum_scatter(
        term().astype(jnp.bfloat16), "row", scatter_dimension=0, tiled=True
    ).astype(jnp.float32)


def join_columns(matrices, col_count):
    pieces = [
        matrix.reshape(matrix.shape[0], col_count, matrix.shape[1] // col_count)
        for matrix in matrices
    ]
    return jnp.concatenate(pieces, axis=2).reshape(matrices[0].shape[0], -1)


def split_columns(joined, widths, col_count):
    shaped = joined.reshape(joined.shape[0], col_count, sum(widths))
    results = []
    offset = 0
    for piece_width in widths:
        results.append(
            shaped[:, :, offset : offset + piece_width].reshape(
                joined.shape[0], col_count * piece_width
            )
        )
        offset += piece_width
    return results


def project_in(rows_full, joined):
    partial_terms = jnp.dot(rows_full, joined, preferred_element_type=jnp.float32)
    return lax.psum_scatter(partial_terms, "col", scatter_dimension=1, tiled=True)


def norm_back(grad_rows, unit_rows, scale_rows, gain, model_width):
    weighted = grad_rows * gain
    inner = col_total(jnp.sum(weighted * unit_rows, axis=1)) / model_width
    return scale_rows * (weighted - unit_rows * inner[:, None])


def head_norm_back(grad_rows, unit_rows, scale_rows, gain):
    weighted = grad_rows * gain
    return scale_rows * (
        weighted - unit_rows * jnp.mean(weighted * unit_rows, axis=-1, keepdims=True)
    )


def allowed_pairs(segments, block_start, block_rows):
    positions = jnp.arange(segments.shape[0], dtype=jnp.int32)
    same_doc = segments[block_start : block_start + block_rows, None] == segments[None, :]
    causal = positions[block_start : block_start + block_rows, None] >= positions[None, :]
    return same_doc & causal


def attention_forward(q_rot, k_rot, v_rows, segments, block_rows):
    length = q_rot.shape[0]
    score_scale = q_rot.shape[-1] ** (-0.5)
    outputs = []
    log_totals = []
    for block_start in range(0, length, block_rows):
        q_block = q_rot[block_start : block_start + block_rows]
        allowed = allowed_pairs(segments, block_start, block_rows)
        scores = (
            jnp.einsum("qkgd,skd->kgqs", q_block, k_rot, preferred_element_type=jnp.float32)
            * score_scale
        )
        scores = jnp.where(allowed, scores, -jnp.inf)
        row_top = jnp.max(scores, axis=-1, keepdims=True)
        log_total = row_top + jnp.log(jnp.sum(jnp.exp(scores - row_top), axis=-1, keepdims=True))
        probs_b = jnp.exp(scores - log_total).astype(jnp.bfloat16)
        outputs.append(
            jnp.einsum("kgqs,skd->qkgd", probs_b, v_rows, preferred_element_type=jnp.float32)
        )
        log_totals.append(log_total)
    return (jnp.concatenate(outputs, axis=0), log_totals)


def attention_backward(q_rot, k_rot, v_rows, segments, log_totals, d_attn, attn_b, block_rows):
    length = q_rot.shape[0]
    score_scale = q_rot.shape[-1] ** (-0.5)
    row_delta = jnp.sum(d_attn.astype(jnp.float32) * attn_b.astype(jnp.float32), axis=-1)
    query_parts = []
    d_krot = jnp.zeros(k_rot.shape, jnp.float32)
    d_value = jnp.zeros(v_rows.shape, jnp.float32)
    for block_index, block_start in enumerate(range(0, length, block_rows)):
        q_block = q_rot[block_start : block_start + block_rows]
        grad_block = d_attn[block_start : block_start + block_rows]
        allowed = allowed_pairs(segments, block_start, block_rows)
        scores = (
            jnp.einsum("qkgd,skd->kgqs", q_block, k_rot, preferred_element_type=jnp.float32)
            * score_scale
        )
        attn_probs = jnp.exp(jnp.where(allowed, scores, -jnp.inf) - log_totals[block_index])
        probs_b = attn_probs.astype(jnp.bfloat16)
        d_probs = jnp.einsum(
            "qkgd,skd->kgqs", grad_block, v_rows, preferred_element_type=jnp.float32
        )
        delta_block = jnp.transpose(row_delta[block_start : block_start + block_rows], (1, 2, 0))[
            ..., None
        ]
        d_scores_b = (attn_probs * (d_probs - delta_block)).astype(jnp.bfloat16)
        query_parts.append(
            jnp.einsum("kgqs,skd->qkgd", d_scores_b, k_rot, preferred_element_type=jnp.float32)
            * score_scale
        )
        d_krot = (
            d_krot
            + jnp.einsum("kgqs,qkgd->skd", d_scores_b, q_block, preferred_element_type=jnp.float32)
            * score_scale
        )
        d_value = d_value + jnp.einsum(
            "kgqs,qkgd->skd", probs_b, grad_block, preferred_element_type=jnp.float32
        )
    return (jnp.concatenate(query_parts, axis=0), d_krot, d_value)


def body(
    block_in,
    out_grad,
    segment_ids,
    attn_gain,
    w_query,
    w_key,
    w_value,
    query_gain,
    key_gain,
    w_out,
    ffn_gain,
    w_gate,
    w_up,
    w_down,
):
    col_count = lax.axis_size("col")
    local_width = block_in.shape[2]
    model_width = local_width * col_count
    stream = block_in[0]
    upstream = out_grad[0]
    segments = segment_ids[0]
    head_width = query_gain.shape[0]
    query_cols = w_query.shape[1] // col_count
    key_cols = w_key.shape[1] // col_count
    value_cols = w_value.shape[1] // col_count
    hidden_cols = w_gate.shape[1] // col_count
    key_heads = key_cols // head_width
    group_size = query_cols // key_cols
    scale_one = lax.rsqrt(col_total(jnp.sum(stream * stream, axis=1)) / model_width + NORM_EPSILON)[
        :, None
    ]
    unit_one = stream * scale_one
    normed_one = (unit_one * attn_gain).astype(jnp.bfloat16)
    rows_one = all_rows(normed_one)
    length = rows_one.shape[0]
    block_rows = min(512, length)
    qkv_joined = join_columns((w_query, w_key, w_value), col_count)
    qkv = project_in(rows_one, qkv_joined)
    query_rows = qkv[:, :query_cols].reshape(length, key_heads * group_size, head_width)
    key_rows = qkv[:, query_cols : query_cols + key_cols].reshape(length, key_heads, head_width)
    value_rows = qkv[:, query_cols + key_cols :].reshape(length, key_heads, head_width)
    cosine, sine = rope_tables(length, head_width)
    q_scale = lax.rsqrt(jnp.mean(query_rows * query_rows, axis=-1, keepdims=True) + NORM_EPSILON)
    q_unit = query_rows * q_scale
    k_scale = lax.rsqrt(jnp.mean(key_rows * key_rows, axis=-1, keepdims=True) + NORM_EPSILON)
    k_unit = key_rows * k_scale
    q_rot = (
        rotate(q_unit * query_gain, cosine, sine, 1.0)
        .astype(jnp.bfloat16)
        .reshape(length, key_heads, group_size, head_width)
    )
    k_rot = rotate(k_unit * key_gain, cosine, sine, 1.0).astype(jnp.bfloat16)
    v_rows = value_rows.astype(jnp.bfloat16)
    attn_rows, log_totals = attention_forward(q_rot, k_rot, v_rows, segments, block_rows)
    attn_b = attn_rows.astype(jnp.bfloat16)
    attn_cols = head_gather(attn_b.reshape(length, query_cols))
    middle = stream + scatter_rows(attn_cols, w_out, False)
    scale_two = lax.rsqrt(col_total(jnp.sum(middle * middle, axis=1)) / model_width + NORM_EPSILON)[
        :, None
    ]
    unit_two = middle * scale_two
    normed_two = (unit_two * ffn_gain).astype(jnp.bfloat16)
    rows_two = all_rows(normed_two)
    gate_joined = join_columns((w_gate, w_up), col_count)
    gate_up = project_in(rows_two, gate_joined)
    gate = gate_up[:, :hidden_cols]
    up_proj = gate_up[:, hidden_cols:]
    sigmoid_gate = jax.nn.sigmoid(gate)
    silu_gate = gate * sigmoid_gate
    activated = (silu_gate * up_proj).astype(jnp.bfloat16)
    act_cols = head_gather(activated)
    block_out = middle + scatter_rows(act_cols, w_down, False)
    grad_b = upstream.astype(jnp.bfloat16)
    grad_rows = all_rows(grad_b)
    d_act = back_sums(times_transposed(grad_rows, w_down))
    grad_down = contract_rows(act_cols, grad_rows)
    d_gate = d_act * up_proj * (sigmoid_gate * (1.0 + gate * (1.0 - sigmoid_gate)))
    d_up = d_act * silu_gate
    d_gate_up = jnp.concatenate([d_gate, d_up], axis=1).astype(jnp.bfloat16)
    d_gate_cols = head_gather(d_gate_up)
    grad_gate, grad_up = split_columns(
        contract_rows(rows_two, d_gate_cols), (hidden_cols, hidden_cols), col_count
    )
    d_normed_two = scatter_rows(d_gate_cols, gate_joined, True)
    gain_two = jnp.sum(d_normed_two * unit_two, axis=0)
    d_middle = upstream + norm_back(d_normed_two, unit_two, scale_two, ffn_gain, model_width)
    middle_b = d_middle.astype(jnp.bfloat16)
    middle_rows = all_rows(middle_b)
    d_attn_f = back_sums(times_transposed(middle_rows, w_out))
    grad_out = contract_rows(attn_cols, middle_rows)
    d_attn = d_attn_f.astype(jnp.bfloat16).reshape(length, key_heads, group_size, head_width)
    d_qrot, d_krot, d_value = attention_backward(
        q_rot, k_rot, v_rows, segments, log_totals, d_attn, attn_b, block_rows
    )
    dq_turn = rotate(d_qrot.reshape(length, key_heads * group_size, head_width), cosine, sine, -1.0)
    dk_turn = rotate(d_krot, cosine, sine, -1.0)
    query_gain_part = jnp.sum(dq_turn * q_unit, axis=(0, 1))
    key_gain_part = jnp.sum(dk_turn * k_unit, axis=(0, 1))
    d_query = head_norm_back(dq_turn, q_unit, q_scale, query_gain)
    d_key = head_norm_back(dk_turn, k_unit, k_scale, key_gain)
    d_qkv = jnp.concatenate(
        [
            d_query.reshape(length, query_cols),
            d_key.reshape(length, key_cols),
            d_value.reshape(length, value_cols),
        ],
        axis=1,
    ).astype(jnp.bfloat16)
    d_qkv_cols = head_gather(d_qkv)
    grad_query, grad_key, grad_value = split_columns(
        contract_rows(rows_one, d_qkv_cols), (query_cols, key_cols, value_cols), col_count
    )
    d_normed_one = scatter_rows(d_qkv_cols, qkv_joined, True)
    gain_one = jnp.sum(d_normed_one * unit_one, axis=0)
    in_grad = d_middle + norm_back(d_normed_one, unit_one, scale_one, attn_gain, model_width)
    grad_query, grad_key, grad_value, grad_out, grad_gate, grad_up, grad_down = (
        lax.psum(grad_query.astype(jnp.bfloat16), "dp").astype(jnp.float32),
        lax.psum(grad_key.astype(jnp.bfloat16), "dp").astype(jnp.float32),
        lax.psum(grad_value.astype(jnp.bfloat16), "dp").astype(jnp.float32),
        lax.psum(grad_out.astype(jnp.bfloat16), "dp").astype(jnp.float32),
        lax.psum(grad_gate.astype(jnp.bfloat16), "dp").astype(jnp.float32),
        lax.psum(grad_up.astype(jnp.bfloat16), "dp").astype(jnp.float32),
        lax.psum(grad_down.astype(jnp.bfloat16), "dp").astype(jnp.float32),
    )
    col_offset = lax.axis_index("col") * local_width
    padded_one = lax.dynamic_update_slice(
        jnp.zeros((model_width,), jnp.float32), gain_one, (col_offset,)
    )
    padded_two = lax.dynamic_update_slice(
        jnp.zeros((model_width,), jnp.float32), gain_two, (col_offset,)
    )
    total_one, total_two, grad_query_gain, grad_key_gain = lax.psum(
        (padded_one, padded_two, query_gain_part, key_gain_part), ("dp", "row", "col")
    )
    grad_attn_gain = lax.dynamic_slice(total_one, (col_offset,), (local_width,))
    grad_ffn_gain = lax.dynamic_slice(total_two, (col_offset,), (local_width,))
    return (
        block_out[None],
        in_grad[None],
        grad_attn_gain,
        grad_query,
        grad_key,
        grad_value,
        grad_query_gain,
        grad_key_gain,
        grad_out,
        grad_ffn_gain,
        grad_gate,
        grad_up,
        grad_down,
    )


def solution(mesh):
    placed = (
        P("dp", "row", "col"),
        P("dp", "row", "col"),
        P("dp", None),
        P("col"),
        P("col", "row"),
        P("col", "row"),
        P("col", "row"),
        P(),
        P(),
        P("row", "col"),
        P("col"),
        P("col", "row"),
        P("col", "row"),
        P("row", "col"),
    )
    return jax.shard_map(
        body,
        mesh=mesh,
        in_specs=placed,
        out_specs=(
            P("dp", "row", "col"),
            P("dp", "row", "col"),
            P("col"),
            P("col", "row"),
            P("col", "row"),
            P("col", "row"),
            P(),
            P(),
            P("row", "col"),
            P("col"),
            P("col", "row"),
            P("col", "row"),
            P("row", "col"),
        ),
        check_vma=False,
    )
```

profile of v0, /device:TPU:0, one launch (start us, length us, event | category | flops | bytes accessed | tf_op | source)
XLA Modules:
  0.0 806.6 jit_solution(5435428760807224259)
XLA Ops:
  7.2 1.3 fusion.67
  8.5 5.9 psum.105
  14.4 1.9 multiply_convert_fusion.4
  19.9 15.1 %all-gather.8.cloned.1.call-done = bf16[1024,512]{1,0:T(8,128)(2,1)} async-done(((bf16[256,512]{1,0:T(8,128)(2,1)}), bf16[1024,512]{1,0:T(8,128)(2,1)}) %all-gather.8.cloned.1.call-update) | async-done | bytes 1048592 | tf_op jit(solution)/shard_map/all_gather | solution.py:38
  34.9 3.3 fusion.96
  40.5 29.8 %reduce-scatter.11.cloned.1.call-done = f32[1024,256]{0,1:T(8,128)} async-done(((f32[1024,512]{0,1:T(8,128)}), f32[1024,256]{0,1:T(8,128)}) %reduce-scatter.11.cloned.1.call-update) | async-done | bytes 1048592 | tf_op jit(solution)/shard_map/reduce_scatter | solution.py:97
  77.4 2.0 exponential_reduce_fusion
  79.5 1.3 convolution_convert_fusion.9
  80.8 1.3 convolution_convert_fusion.8
  82.2 8.7 %all_gather.25 = bf16[1024,256]{0,1:T(8,128)(2,1)S(1)} all-gather(bf16[1024,128]{0,1:T(8,128)(2,1)S(1)} %pad_maximum_fusion.5), channel_id=1, replica_groups=mesh['dp'=4,'row'=4,'col'=2] {'col'}, dimensions={1}, use_global_device_ids=true | all-gather | bytes 786432 | tf_op jit(solution)/shard_map/all_gather | solution.py:42
  90.9 1.4 convolution_convert_fusion.4
  92.4 1.8 bitcast_convert_fusion
  94.2 23.0 %reduce-scatter.13.cloned.1.call-done = bf16[256,512]{1,0:T(8,128)(2,1)} async-done(((bf16[1024,512]{1,0:T(8,128)(2,1)}), bf16[256,512]{1,0:T(8,128)(2,1)}) %reduce-scatter.13.cloned.1.call-update) | async-done | bytes 262160 | tf_op jit(solution)/shard_map/reduce_scatter | solution.py:68
  118.4 4.9 psum.106
  123.3 1.8 multiply_convert_fusion.3
  125.3 10.7 %all-gather.14.cloned.1.call-done = bf16[1024,512]{1,0:T(8,128)(2,1)} async-done(((bf16[256,512]{1,0:T(8,128)(2,1)}), bf16[1024,512]{1,0:T(8,128)(2,1)}) %all-gather.14.cloned.1.call-update) | async-done | bytes 1048592 | tf_op jit(solution)/shard_map/all_gather | solution.py:38
  136.0 4.8 convolution_bitcast_fusion
  140.9 2.4 copy.154
  143.2 2.4 copy.155
  145.6 3.2 pad_maximum_fusion
  148.8 5.9 all-gather.10.cloned.1.call-done
  154.7 8.4 %fusion.97 = f32[1024,2304]{1,0:T(8,128)} fusion(bf16[1024,512]{1,0:T(8,128)(2,1)} %all-gather.10.cloned.1.call-done, bf16[512,2304]{0,1:T(8,128)(2,1)} %bitcast.293), kind=kOutput, calls=%fused_computation.160 | convolution fusion | flops 2415919104 | bytes 12845056 | tf_op jit(solution)/shard_map/dot_general | solution.py:96
  163.2 53.8 %reduce-scatter.25.cloned.1.call-done = f32[576,1024]{1,0:T(8,128)} async-done(((f32[1152,1024]{1,0:T(8,128)}), f32[576,1024]{1,0:T(8,128)}) %reduce-scatter.25.cloned.1.call-update) | async-done | bytes 2359312
  217.0 3.1 copy.185
  220.1 109.8 %reduce-scatter.15.cloned.1.call-done = f32[1024,1152]{1,0:T(8,128)} async-done(((f32[1024,2304]{1,0:T(8,128)}), f32[1024,1152]{1,0:T(8,128)}) %reduce-scatter.15.cloned.1.call-update) | async-done | bytes 4718608 | tf_op jit(solution)/shard_map/reduce_scatter | solution.py:97
  329.9 4.9 multiply_convert_fusion.1
  334.9 2.2 pad_maximum_fusion.1
  337.1 62.7 %all-gather.16.cloned.1.call-done = bf16[1024,2304]{1,0:T(8,128)(2,1)} async-done(((bf16[1024,1152]{1,0:T(8,128)(2,1)}), bf16[1024,2304]{1,0:T(8,128)(2,1)}) %all-gather.16.cloned.1.call-update) | async-done | bytes 4718608 | tf_op jit(solution)/shard_map/all_gather | solution.py:42
  399.8 6.7 convolution_convert_fusion.2
  406.6 24.9 %reduce-scatter.19.cloned.1.call-done = bf16[256,512]{1,0:T(8,128)(2,1)} async-done(((bf16[1024,512]{1,0:T(8,128)(2,1)}), bf16[256,512]{1,0:T(8,128)(2,1)}) %reduce-scatter.19.cloned.1.call-update) | async-done | bytes 262160 | tf_op jit(solution)/shard_map/reduce_scatter | solution.py:68
  431.5 1.8 fusion.62
  433.3 5.6 psum.107
  440.1 2.0 fusion.83
  442.2 16.8 %all-gather.18.cloned.1.call-done = bf16[1024,512]{1,0:T(8,128)(2,1)} async-done(((bf16[256,512]{1,0:T(8,128)(2,1)}), bf16[1024,512]{1,0:T(8,128)(2,1)}) %all-gather.18.cloned.1.call-update) | async-done | bytes 1048592 | tf_op jit(solution)/shard_map/all_gather | solution.py:38
  459.0 2.7 fusion.98
  462.0 1.2 mul.634
  463.2 1.3 mul.635
  464.5 17.8 %reduce-scatter.21.cloned.1.call-done = f32[1024,128]{1,0:T(8,128)} async-done(((f32[1024,256]{1,0:T(8,128)}), f32[1024,128]{1,0:T(8,128)}) %reduce-scatter.21.cloned.1.call-update) | async-done | bytes 524304 | tf_op jit(solution)/shard_map/reduce_scatter | solution.py:46
  482.3 1.8 convert_element_type.164
  484.0 1.9 copy.159
  485.9 1.7 fusion.90
  489.4 1.7 copy.158
  491.1 3.9 fusion.3
  496.2 1.5 fusion.33
  497.7 2.0 convolution_bitcast_fusion.2
  499.7 1.7 copy.161
  501.4 3.9 fusion.1
  508.8 1.3 fusion.50
  511.4 2.4 copy.156
  513.8 18.9 %all-gather.20.cloned.1.call-done = bf16[1024,512]{0,1:T(8,128)(2,1)} async-done(((bf16[1024,256]{0,1:T(8,128)(2,1)}), bf16[1024,512]{0,1:T(8,128)(2,1)}) %all-gather.20.cloned.1.call-update) | async-done | bytes 1048592 | tf_op jit(solution)/shard_map/all_gather | solution.py:42
  532.7 3.0 convolution_convert_fusion.5
  535.9 35.1 %all-gather.12.cloned.1.call-done = bf16[1024,1152]{0,1:T(8,128)(2,1)} async-done(((bf16[1024,576]{0,1:T(8,128)(2,1)}), bf16[1024,1152]{0,1:T(8,128)(2,1)}) %all-gather.12.cloned.1.call-update) | async-done | bytes 2359312 | tf_op jit(solution)/shard_map/all_gather | solution.py:42
  570.9 4.2 convolution_convert_fusion.3
  575.5 4.3 convolution_convert_fusion.1
  579.8 6.4 convolution_convert_fusion
  586.2 4.3 copy.186
  590.5 3.3 fusion.88
  599.7 39.4 %all-reduce = (f32[1024]{0:T(1024)S(1)}, f32[64]{0:T(128)}, f32[64]{0:T(128)}, f32[1024]{0:T(1024)S(1)}) all-reduce(f32[1024]{0:T(1024)S(1)} %dynamic_update_slice.6, f32[64]{0:T(128)S(1)} %reduce_sum.156, f32[64]{0:T(128)S(1)} %copy-done.67, ...), channel_id=1, replica_groups=mesh['dp'=4,'row'=4,'col'=2] {'dp','row','col'}, use_global_device_ids=true, to_apply=%region_26.27 | all-reduce | flops 2176 | bytes 17408 | tf_op jit(solution)/shard_map/psum | solution.py:314
  640.4 5.2 psum.108
  645.6 2.3 fusion.58
  647.9 140.9 %all-reduce.4.cloned.1.call-done = (bf16[512,128]{0,1:T(8,128)(2,1)}, bf16[512,128]{0,1:T(8,128)(2,1)}, bf16[512,1152]{0,1:T(8,128)(2,1)}, bf16[512,1152]{0,1:T(...) async-done(((bf16[512,128]{0,1:T(8,128)(2,1)}, bf16[512,128]{0,1:T(8,128)(2,1)}, bf16[512,1152]{0,1:T(8,128)(2,1)}, ...) | async-done | bytes 4325392 | tf_op jit(solution)/shard_map/psum | solution.py:300
  788.8 3.0 convert_element_type.185
  791.8 2.8 copy.172
  794.6 1.7 copy.173
  (244 shorter events, 34.4 us)
Async XLA Ops:
  7.2 128.8 %copy-start = (bf16[1152,512]{1,0:T(8,128)(2,1)S(1)}, bf16[1152,512]{1,0:T(8,128)(2,1)}, u32[]{:S(2)}) copy-start(bf16[1152,512]{1,0:T(8,128)(2,1)} %param.27) | copy-start | bytes 3538948
  7.2 11.5 %copy-start.42 = (bf16[512,256]{1,0:T(8,128)(2,1)S(1)}, bf16[512,256]{1,0:T(8,128)(2,1)}, u32[]{:S(2)}) copy-start(bf16[512,256]{1,0:T(8,128)(2,1)} %param.18) | copy-start | bytes 786436
  7.2 27.7 %all-gather.8.cloned.1.call-start = ((), (), s32[]{:S(2)}) async-start(), calls=%async_computation.8 | async-start | bytes 1310720 | tf_op jit(solution)/shard_map/all_gather | solution.py:38
  14.4 3.0 copy-start.51
  16.3 54.1 %reduce-scatter.11.cloned.1.call-start = ((), (), s32[]{:S(2)}) async-start(), calls=%async_computation.9 | async-start | bytes 3145728 | tf_op jit(solution)/shard_map/reduce_scatter | solution.py:97
  19.8 18.4 %copy-start.11 = (bf16[64,8,2,256]{3,1,2,0:T(8,128)(2,1)}, bf16[64,8,2,256]{3,1,2,0:T(8,128)(2,1)S(1)}, u32[]{:S(2)}) copy-start(bf16[64,8,2,256]{3,1,2,0:T(8,128)(2,1)S(1)} %copy.187) | copy-start | bytes 1572868
  34.9 3.5 copy-start.53
  38.3 34.2 %copy-start.59 = (f32[64]{0:T(128)S(1)}, f32[64]{0:T(128)}, u32[]{:S(2)}) copy-start(f32[64]{0:T(128)} %param.22) | copy-start | bytes 772
  38.3 35.8 %copy-start.65 = (f32[64]{0:T(128)S(1)}, f32[64]{0:T(128)}, u32[]{:S(2)}) copy-start(f32[64]{0:T(128)} %param.21) | copy-start | bytes 772
  38.3 79.0 %reduce-scatter.13.cloned.1.call-start = ((), (), s32[]{:S(2)}) async-start(), calls=%async_computation.10 | async-start | bytes 1310720 | tf_op jit(solution)/shard_map/reduce_scatter | solution.py:68
  38.4 37.0 %copy-start.57 = (f32[32]{0:T(128)}, f32[32]{0:T(128)S(1)}, u32[]{:S(2)}) copy-start(f32[32]{0:T(128)S(1)} %negate_power_fusion) | copy-start | bytes 388
  39.6 36.8 %copy-start.24 = (f32[1024,32]{0,1:T(8,128)}, f32[1024,32]{0,1:T(8,128)S(1)}, u32[]{:S(2)}) copy-start(f32[1024,32]{0,1:T(8,128)S(1)} %get-tuple-element.100) | copy-start | bytes 393220
  40.5 39.0 %copy-start.15 = (pred[512,1024]{0,1:T(8,128)(4,1)}, pred[512,1024]{0,1:T(8,128)(4,1)S(1)}, u32[]{:S(2)}) copy-start(pred[512,1024]{0,1:T(8,128)(4,1)S(1)} %get-tuple-element.94) | copy-start | bytes 1572868
  40.5 40.3 %copy-start.13 = (pred[512,1024]{0,1:T(8,128)(4,1)}, pred[512,1024]{0,1:T(8,128)(4,1)S(1)}, u32[]{:S(2)}) copy-start(pred[512,1024]{0,1:T(8,128)(4,1)S(1)} %get-tuple-element.95) | copy-start | bytes 1572868
  76.4 3.1 copy-start.8
  77.4 3.4 copy-start.6
  80.8 10.0 %copy-start.27 = (bf16[256,512]{1,0:T(8,128)(2,1)S(1)}, bf16[256,512]{1,0:T(8,128)(2,1)}, u32[]{:S(2)}) copy-start(bf16[256,512]{1,0:T(8,128)(2,1)} %param.23) | copy-start | bytes 786436
  82.1 8.7 %copy-start.39 = (bf16[64,2,512]{2,0,1:T(8,128)(2,1)}, bf16[64,2,512]{2,0,1:T(8,128)(2,1)S(1)}, u32[]{:S(2)}) copy-start(bf16[64,2,512]{2,0,1:T(8,128)(2,1)S(1)} %convolution_convert_fusion.8) | copy-start | bytes 393220
  82.1 35.1 %copy-start.1 = (f32[1,256,512]{2,1,0:T(8,128)S(1)}, f32[1,256,512]{2,1,0:T(8,128)}, u32[]{:S(2)}) copy-start(f32[1,256,512]{2,1,0:T(8,128)} %param.14) | copy-start | bytes 1572868
  82.2 41.1 %copy-start.47 = (f32[512]{0:T(512)S(1)}, f32[512]{0:T(512)}, u32[]{:S(2)}) copy-start(f32[512]{0:T(512)} %param.24) | copy-start | bytes 6148
  92.3 43.7 %all-gather.14.cloned.1.call-start = ((), (), s32[]{:S(2)}) async-start(), calls=%async_computation.15 | async-start | bytes 1310720 | tf_op jit(solution)/shard_map/all_gather | solution.py:38
  94.2 60.5 %all-gather.10.cloned.1.call-start = ((), (), s32[]{:S(2)}) async-start(), calls=%async_computation.11 | async-start | bytes 1310720 | tf_op jit(solution)/shard_map/all_gather | solution.py:38
  123.3 17.5 %copy-start.48 = (f32[256]{0:T(256)}, f32[256]{0:T(256)S(1)}, u32[]{:S(2)}) copy-start(f32[256]{0:T(256)S(1)} %add_rsqrt_fusion.2) | copy-start | bytes 3076
  125.1 91.8 %reduce-scatter.25.cloned.1.call-start = ((), (), s32[]{:S(2)}) async-start(), calls=%async_computation.22 | async-start | bytes 7077888
  140.8 189.1 %reduce-scatter.15.cloned.1.call-start = ((), (), s32[]{:S(2)}) async-start(), calls=%async_computation.12 | async-start | bytes 14155776 | tf_op jit(solution)/shard_map/reduce_scatter | solution.py:97
  163.1 236.7 %all-gather.16.cloned.1.call-start = ((), (), s32[]{:S(2)}) async-start(), calls=%async_computation.16 | async-start | bytes 7077888 | tf_op jit(solution)/shard_map/all_gather | solution.py:42
  337.0 94.4 %copy-start.3 = (bf16[256,512]{1,0:T(8,128)(2,1)S(1)}, bf16[256,512]{1,0:T(8,128)(2,1)}, u32[]{:S(2)}) copy-start(bf16[256,512]{1,0:T(8,128)(2,1)} %reduce-scatter.13.cloned.1.call-done) | copy-start | bytes 786436
  337.0 94.4 %reduce-scatter.19.cloned.1.call-start = ((), (), s32[]{:S(2)}) async-start(), calls=%async_computation.17 | async-start | bytes 1310720 | tf_op jit(solution)/shard_map/reduce_scatter | solution.py:68
  406.5 52.5 %all-gather.18.cloned.1.call-start = ((), (), s32[]{:S(2)}) async-start(), calls=%async_computation.18 | async-start | bytes 1310720 | tf_op jit(solution)/shard_map/all_gather | solution.py:38
  442.2 40.1 %reduce-scatter.21.cloned.1.call-start = ((), (), s32[]{:S(2)}) async-start(), calls=%async_computation.19 | async-start | bytes 1572864 | tf_op jit(solution)/shard_map/reduce_scatter | solution.py:46
  461.7 71.0 %all-gather.20.cloned.1.call-start = ((), (), s32[]{:S(2)}) async-start(), calls=%async_computation.20 | async-start | bytes 1572864 | tf_op jit(solution)/shard_map/all_gather | solution.py:42
  491.0 3.9 copy-start.32
  491.0 3.9 copy-start.35
  491.1 5.1 copy-start.19
  491.1 5.1 copy-start.22
  495.0 2.7 copy-start.9
  495.0 2.7 copy-start.16
  495.0 2.7 copy-start.46
  495.0 2.7 copy-start.64
  501.4 3.9 copy-start.33
  501.4 3.9 copy-start.36
  506.4 2.3 copy-start.45
  506.4 2.4 copy-start.71
  510.4 22.3 %copy-start.12 = (bf16[64,8,2,256]{3,1,2,0:T(8,128)(2,1)S(1)}, bf16[64,8,2,256]{3,1,2,0:T(8,128)(2,1)}, u32[]{:S(2)}) copy-start(bf16[64,8,2,256]{3,1,2,0:T(8,128)(2,1)} %copy-done.11) | copy-start | bytes 1572868
  511.3 59.6 %all-gather.12.cloned.1.call-start = ((), (), s32[]{:S(2)}) async-start(), calls=%async_computation.13 | async-start | bytes 3538944 | tf_op jit(solution)/shard_map/all_gather | solution.py:42
  513.8 84.4 %reduce-scatter.23.cloned.1.call-start = ((), (), s32[]{:S(2)}) async-start(), calls=%async_computation.21 | async-start | bytes 1310720 | tf_op jit(solution)/shard_map/reduce_scatter | solution.py:68
  535.8 39.7 %copy-start.29 = (bf16[1024,512]{1,0:T(8,128)(2,1)S(1)}, bf16[1024,512]{1,0:T(8,128)(2,1)}, u32[]{:S(2)}) copy-start(bf16[1024,512]{1,0:T(8,128)(2,1)} %all-gather.14.cloned.1.call-done) | copy-start | bytes 3145732
  535.8 109.7 %reduce-scatter.17.cloned.1.call-start = ((), (), s32[]{:S(2)}) async-start(), calls=%async_computation.14 | async-start | bytes 1310720 | tf_op jit(solution)/shard_map/reduce_scatter | solution.py:68
  575.2 213.6 %all-reduce.4.cloned.1.call-start = ((), (), s32[]{:S(2)}) async-start(), calls=%async_computation.23 | async-start | bytes 8650752 | tf_op jit(solution)/shard_map/psum | solution.py:300
  575.5 4.3 copy-start.69
  590.5 3.3 copy-start.5
  590.5 4.5 copy-start.26
  590.5 4.5 copy-start.70
  595.7 2.5 copy-start.50
  595.7 2.4 copy-start.52
  597.3 2.3 copy-start.67
  597.3 48.2 %copy-start.4 = (f32[1,256,512]{2,1,0:T(8,128)S(1)}, f32[1,256,512]{2,1,0:T(8,128)}, u32[]{:S(2)}) copy-start(f32[1,256,512]{2,1,0:T(8,128)} %param.15) | copy-start | bytes 1572868
  597.3 48.2 %copy-start.10 = (bf16[256,512]{1,0:T(8,128)(2,1)S(1)}, bf16[256,512]{1,0:T(8,128)(2,1)}, u32[]{:S(2)}) copy-start(bf16[256,512]{1,0:T(8,128)(2,1)} %reduce-scatter.19.cloned.1.call-done) | copy-start | bytes 786436
  597.3 48.2 %copy-start.49 = (f32[256]{0:T(256)S(1)}, f32[256]{0:T(256)}, u32[]{:S(2)}) copy-start(f32[256]{0:T(256)} %copy-done.48) | copy-start | bytes 3076
  597.3 48.2 %copy-start.55 = (f32[256]{0:T(256)S(1)}, f32[256]{0:T(256)}, u32[]{:S(2)}) copy-start(f32[256]{0:T(256)} %copy-done.54) | copy-start | bytes 3076
  791.8 2.8 copy-start.17
  794.6 2.6 copy-start.40
  794.6 3.5 copy-start.44
  794.6 4.3 copy-start.43
  (24 other events, 36.0 us)
Sparse Core Ops, SparseCore 0:
  16.4 18.4 all-gather.7
  38.4 31.8 reduce-scatter.10
  92.5 24.7 reduce-scatter.12
  119.3 16.6 all-gather.13
  138.0 16.6 all-gather.9
  156.9 60.0 reduce-scatter.24
  219.3 110.6 reduce-scatter.14
  337.2 62.6 all-gather.15
  406.6 24.7 reduce-scatter.18
  442.3 16.6 all-gather.17
  461.9 20.3 reduce-scatter.20
  511.4 21.2 all-gather.19
  534.9 36.0 all-gather.11
  573.3 24.8 reduce-scatter.22
  600.5 24.8 reduce-scatter.16
  629.3 159.4 all-reduce.3
where the time goes:
time: 816 us; the launch traced here: 807 us
  waiting for transfers between devices  566 us (69%)
  blocking collectives  69.6 us (9%)
  matrix products  66.4 us (8%)
  other arithmetic  46.4 us (6%)
  local copies, waits for them, and re-layouts  41.5 us (5%)
  between operations  15.4 us (2%)
    psum x1, waiting for transfers between devices, body(): lax.psum(grad_key.astype(jnp.bfloat16), 'dp').astype(jnp.float32)  141 us
    reduce_scatter x2, waiting for transfers between devices, project_in(): lax.psum_scatter(partial_terms, 'col', scatter_dimension=1, tiled=True)  140 us
    all_gather x3, waiting for transfers between devices, head_gather(): return lax.all_gather(local_part, 'col', axis=1, tiled=True)  117 us
    unnamed x17, waiting for transfers between devices  54.1 us
    all_gather x4, waiting for transfers between devices, all_rows(): return lax.all_gather(local_part, 'row', axis=0, tiled=True)  48.5 us
    reduce_scatter x4, waiting for transfers between devices, scatter_rows(): lax.psum_scatter(term().astype(jnp.bfloat16), 'row', scatter_dimension=0,...  48.4 us
    psum x1, blocking collectives, body(): lax.psum((padded_one, padded_two, query_gain_part, key_gain_part), ('dp',...  39.4 us
    psum x4, blocking collectives, col_total(): return lax.psum(values, 'col')  21.5 us
  transfers between devices with their start and end apart: 16, of which 15 were waited for; matrix products, arithmetic and copies ran while one was open for 9% of the time, Pallas kernels for 0%

commit v1 on v0

v1 whole, which is shorter than its diff:
```python
import jax
import jax.numpy as jnp
from jax import lax
from jax.sharding import PartitionSpec as P

NORM_EPSILON = 1e-05
ROPE_BASE = 1000000.0
F32 = jnp.float32
BF16 = jnp.bfloat16


def rope_tables(length, head_width):
    half_width = head_width // 2
    exponents = jnp.arange(half_width, dtype=jnp.float32) * (2.0 / head_width)
    frequency = ROPE_BASE ** (-exponents)
    angles = jnp.arange(length, dtype=jnp.float32)[:, None] * frequency[None, :]
    return (jnp.cos(angles), jnp.sin(angles))


def rotate(vectors, cosine, sine, direction):
    half_width = vectors.shape[-1] // 2
    first_half = vectors[..., :half_width]
    second_half = vectors[..., half_width:]
    cos_rows = cosine[:, None, :]
    sin_rows = sine[:, None, :] * direction
    return jnp.concatenate(
        [
            first_half * cos_rows - second_half * sin_rows,
            second_half * cos_rows + first_half * sin_rows,
        ],
        axis=-1,
    )


def swap(values, axis, bit):
    count = lax.axis_size(axis)
    return lax.ppermute(values, axis, [(i, i ^ bit) for i in range(count)])


def bits_of(axis):
    count = lax.axis_size(axis)
    bits = []
    while count > 1:
        count //= 2
        bits.append(count)
    return bits


def row_order():
    order = [0]
    for bit in bits_of("row"):
        order = order + [j ^ bit for j in order]
    return order


def together(values):
    return lax.optimization_barrier(values)


def grow(block, axis, bit, dim):
    return jnp.concatenate([block, swap(block, axis, bit)], axis=dim)


def grow_both(one, one_step, two, two_step):
    got_one = swap(one, one_step[0], one_step[1])
    got_two = swap(two, two_step[0], two_step[1])
    got_one, got_two = together((got_one, got_two))
    return (
        jnp.concatenate([one, got_one], axis=one_step[2]),
        jnp.concatenate([two, got_two], axis=two_step[2]),
    )


def gather_all(block):
    col_steps = [("col", bit, 1) for bit in reversed(bits_of("col"))]
    row_steps = [("row", bit, 0) for bit in bits_of("row")]
    far, near = row_steps[:-1], row_steps[-1:]
    half = block.shape[0] // 2
    one, two = block[:half], block[half:]
    steps_one, steps_two = col_steps + far, far + col_steps
    for step_one, step_two in zip(steps_one, steps_two):
        one, two = grow_both(one, step_one, two, step_two)
    width = one.shape[1]
    full = jnp.concatenate(
        [one.reshape(-1, half, width), two.reshape(-1, half, width)], axis=1
    ).reshape(-1, width)
    for axis, bit, dim in near:
        full = grow(full, axis, bit, dim)
    return full


def halves(values, dim):
    middle = values.shape[dim] // 2
    if dim == 0:
        return values[:middle], values[middle:]
    return values[:, :middle], values[:, middle:]


def fold(values, axis, bit, dim):
    keep, give = halves(values, dim)
    return keep + swap(give.astype(BF16), axis, bit).astype(F32)


def fold_both(one, one_step, two, two_step):
    keep_one, give_one = halves(one, one_step[2])
    keep_two, give_two = halves(two, two_step[2])
    got_one = swap(give_one.astype(BF16), one_step[0], one_step[1])
    got_two = swap(give_two.astype(BF16), two_step[0], two_step[1])
    got_one, got_two = together((got_one, got_two))
    return keep_one + got_one.astype(F32), keep_two + got_two.astype(F32)


def scatter_all(terms):
    col_steps = [("col", bit, 1) for bit in bits_of("col")]
    row_steps = [("row", bit, 0) for bit in reversed(bits_of("row"))]
    near, far = row_steps[:1], row_steps[1:]
    for axis, bit, dim in near:
        terms = fold(terms, axis, bit, dim)
    rows = terms.shape[0] * len(near) * 2 // lax.axis_size("row")
    half, width = rows // 2, terms.shape[1]
    split = terms.reshape(-1, 2, half, width)
    one = split[:, 0].reshape(-1, width)
    two = split[:, 1].reshape(-1, width)
    steps_one, steps_two = far + col_steps, col_steps + far
    for step_one, step_two in zip(steps_one, steps_two):
        one, two = fold_both(one, step_one, two, step_two)
    return jnp.concatenate([one, two], axis=0)


def scatter_rows(terms):
    for bit in reversed(bits_of("row")):
        terms = fold(terms, "row", bit, 0)
    return terms


def col_gather(values, dim):
    for bit in reversed(bits_of("col")):
        values = grow(values, "col", bit, dim)
    return values


def col_total(values):
    for bit in bits_of("col"):
        values = values + swap(values, "col", bit)
    return values


def all_total(values, axes):
    for axis in axes:
        for bit in reversed(bits_of(axis)):
            values = values + swap(values, axis, bit)
    return values


def col_pieces(matrices, dim):
    count = lax.axis_size("col")
    index = lax.axis_index("col")
    pieces = []
    for offset in range(count):
        member = index ^ offset
        cut = []
        for matrix in matrices:
            width = matrix.shape[dim] // count
            cut.append(lax.dynamic_slice_in_dim(matrix, member * width, width, dim))
        pieces.append(jnp.concatenate(cut, axis=1) if len(cut) > 1 else cut[0])
    return pieces


def regroup(pieces, dim):
    got = [pieces[0]] + [
        swap(piece, "col", offset) for offset, piece in enumerate(pieces) if offset
    ]
    return jnp.concatenate(got, axis=dim)


def natural_cols(blocks, dim):
    index = lax.axis_index("col")
    count = len(blocks)
    stacked = jnp.stack(blocks)
    return jnp.concatenate(
        [
            lax.dynamic_index_in_dim(stacked, index ^ place, 0, keepdims=False)
            for place in range(count)
        ],
        axis=dim,
    )


def relative_rows(values, order):
    index = lax.axis_index("row")
    rows = values.shape[0] // len(order)
    return jnp.concatenate(
        [
            lax.dynamic_slice_in_dim(values, (index ^ offset) * rows, rows, 0)
            for offset in order
        ],
        axis=0,
    )


def contract_rows(left, right):
    return lax.dot_general(
        left, right, (((0,), (0,)), ((), ())), preferred_element_type=jnp.float32
    )


def times_transposed(left, right):
    return lax.dot_general(
        left, right, (((1,), (1,)), ((), ())), preferred_element_type=jnp.float32
    )


def times(left, right):
    return jnp.dot(left, right, preferred_element_type=jnp.float32)


def norm_back(grad_rows, unit_rows, scale_rows, gain, model_width):
    weighted = grad_rows * gain
    inner = col_total(jnp.sum(weighted * unit_rows, axis=1)) / model_width
    return scale_rows * (weighted - unit_rows * inner[:, None])


def head_norm_back(grad_rows, unit_rows, scale_rows, gain):
    weighted = grad_rows * gain
    return scale_rows * (
        weighted - unit_rows * jnp.mean(weighted * unit_rows, axis=-1, keepdims=True)
    )


def allowed_pairs(segments, positions, block_start, block_rows):
    rows = slice(block_start, block_start + block_rows)
    same_doc = segments[rows, None] == segments[None, :]
    causal = positions[rows, None] >= positions[None, :]
    return same_doc & causal


def attention_forward(q_rot, k_rot, v_rows, segments, positions, block_rows):
    length = q_rot.shape[0]
    score_scale = q_rot.shape[-1] ** (-0.5)
    outputs = []
    log_totals = []
    for block_start in range(0, length, block_rows):
        q_block = q_rot[block_start : block_start + block_rows]
        allowed = allowed_pairs(segments, positions, block_start, block_rows)
        scores = (
            jnp.einsum("qkgd,skd->kgqs", q_block, k_rot, preferred_element_type=jnp.float32)
            * score_scale
        )
        scores = jnp.where(allowed, scores, -jnp.inf)
        row_top = jnp.max(scores, axis=-1, keepdims=True)
        log_total = row_top + jnp.log(jnp.sum(jnp.exp(scores - row_top), axis=-1, keepdims=True))
        probs_b = jnp.exp(scores - log_total).astype(jnp.bfloat16)
        outputs.append(
            jnp.einsum("kgqs,skd->qkgd", probs_b, v_rows, preferred_element_type=jnp.float32)
        )
        log_totals.append(log_total)
    return (jnp.concatenate(outputs, axis=0), log_totals)


def attention_backward(q_rot, k_rot, v_rows, segments, positions, log_totals, d_attn, attn_b, block_rows):
    length = q_rot.shape[0]
    score_scale = q_rot.shape[-1] ** (-0.5)
    row_delta = jnp.sum(d_attn.astype(jnp.float32) * attn_b.astype(jnp.float32), axis=-1)
    query_parts = []
    d_krot = jnp.zeros(k_rot.shape, jnp.float32)
    d_value = jnp.zeros(v_rows.shape, jnp.float32)
    for block_index, block_start in enumerate(range(0, length, block_rows)):
        q_block = q_rot[block_start : block_start + block_rows]
        grad_block = d_attn[block_start : block_start + block_rows]
        allowed = allowed_pairs(segments, positions, block_start, block_rows)
        scores = (
            jnp.einsum("qkgd,skd->kgqs", q_block, k_rot, preferred_element_type=jnp.float32)
            * score_scale
        )
        attn_probs = jnp.exp(jnp.where(allowed, scores, -jnp.inf) - log_totals[block_index])
        probs_b = attn_probs.astype(jnp.bfloat16)
        d_probs = jnp.einsum(
            "qkgd,skd->kgqs", grad_block, v_rows, preferred_element_type=jnp.float32
        )
        delta_block = jnp.transpose(row_delta[block_start : block_start + block_rows], (1, 2, 0))[
            ..., None
        ]
        d_scores_b = (attn_probs * (d_probs - delta_block)).astype(jnp.bfloat16)
        query_parts.append(
            jnp.einsum("kgqs,skd->qkgd", d_scores_b, k_rot, preferred_element_type=jnp.float32)
            * score_scale
        )
        d_krot = (
            d_krot
            + jnp.einsum("kgqs,qkgd->skd", d_scores_b, q_block, preferred_element_type=jnp.float32)
            * score_scale
        )
        d_value = d_value + jnp.einsum(
            "kgqs,qkgd->skd", probs_b, grad_block, preferred_element_type=jnp.float32
        )
    return (jnp.concatenate(query_parts, axis=0), d_krot, d_value)


def body(
    block_in,
    out_grad,
    segment_ids,
    attn_gain,
    w_query,
    w_key,
    w_value,
    query_gain,
    key_gain,
    w_out,
    ffn_gain,
    w_gate,
    w_up,
    w_down,
):
    col_count = lax.axis_size("col")
    local_width = block_in.shape[2]
    model_width = local_width * col_count
    stream = block_in[0]
    upstream = out_grad[0]
    head_width = query_gain.shape[0]
    query_cols = w_query.shape[1] // col_count
    key_cols = w_key.shape[1] // col_count
    value_cols = w_value.shape[1] // col_count
    hidden_cols = w_gate.shape[1] // col_count
    key_heads = key_cols // head_width
    group_size = query_cols // key_cols
    order = row_order()

    scale_one = lax.rsqrt(col_total(jnp.sum(stream * stream, axis=1)) / model_width + NORM_EPSILON)[
        :, None
    ]
    unit_one = stream * scale_one
    normed_one = (unit_one * attn_gain).astype(BF16)
    rows_one = gather_all(normed_one)
    length = rows_one.shape[0]
    block_rows = min(512, length)

    qkv_pieces = col_pieces((w_query, w_key, w_value), 1)
    qkv_own = regroup(qkv_pieces, 0)
    qkv_local = jnp.concatenate(qkv_pieces, axis=1)
    out_pieces = col_pieces((w_out,), 0)
    out_own = regroup(out_pieces, 1)
    out_local = jnp.concatenate(out_pieces, axis=0)
    gate_own = regroup(col_pieces((w_gate, w_up), 1), 0)
    down_own = regroup(col_pieces((w_down,), 0), 1)
    grad_rows = gather_all(upstream.astype(BF16))

    segments = relative_rows(segment_ids[0], order)
    positions = relative_rows(jnp.arange(length, dtype=jnp.int32), order)
    cosine, sine = rope_tables(length, head_width)
    cosine, sine = relative_rows(cosine, order), relative_rows(sine, order)

    qkv = times(rows_one, qkv_own)
    query_rows = qkv[:, :query_cols].reshape(length, key_heads * group_size, head_width)
    key_rows = qkv[:, query_cols : query_cols + key_cols].reshape(length, key_heads, head_width)
    value_rows = qkv[:, query_cols + key_cols :].reshape(length, key_heads, head_width)
    q_scale = lax.rsqrt(jnp.mean(query_rows * query_rows, axis=-1, keepdims=True) + NORM_EPSILON)
    q_unit = query_rows * q_scale
    k_scale = lax.rsqrt(jnp.mean(key_rows * key_rows, axis=-1, keepdims=True) + NORM_EPSILON)
    k_unit = key_rows * k_scale
    q_rot = (
        rotate(q_unit * query_gain, cosine, sine, 1.0)
        .astype(BF16)
        .reshape(length, key_heads, group_size, head_width)
    )
    k_rot = rotate(k_unit * key_gain, cosine, sine, 1.0).astype(BF16)
    v_rows = value_rows.astype(BF16)
    attn_rows, log_totals = attention_forward(q_rot, k_rot, v_rows, segments, positions, block_rows)
    attn_b = attn_rows.astype(BF16)
    attn_cols = col_gather(attn_b.reshape(length, query_cols), 1)
    middle = stream + scatter_rows(times(attn_cols, out_local))
    scale_two = lax.rsqrt(col_total(jnp.sum(middle * middle, axis=1)) / model_width + NORM_EPSILON)[
        :, None
    ]
    unit_two = middle * scale_two
    normed_two = (unit_two * ffn_gain).astype(BF16)
    rows_two = gather_all(normed_two)
    gate_up = times(rows_two, gate_own)
    gate = gate_up[:, :hidden_cols]
    up_proj = gate_up[:, hidden_cols:]
    sigmoid_gate = jax.nn.sigmoid(gate)
    silu_gate = gate * sigmoid_gate
    activated = (silu_gate * up_proj).astype(BF16)
    d_act = times_transposed(grad_rows, down_own)
    d_gate = d_act * up_proj * (sigmoid_gate * (1.0 + gate * (1.0 - sigmoid_gate)))
    d_up = d_act * silu_gate
    d_gate_up = jnp.concatenate([d_gate, d_up], axis=1).astype(BF16)

    down_terms = contract_rows(activated, grad_rows).astype(BF16)
    gate_terms = jnp.concatenate(
        [
            contract_rows(rows_two[:, k * local_width : (k + 1) * local_width], d_gate_up)
            for k in range(col_count)
        ],
        axis=1,
    ).astype(BF16)
    down_part = lax.psum_scatter(down_terms, "dp", scatter_dimension=0, tiled=True)
    gate_part = lax.psum_scatter(gate_terms, "dp", scatter_dimension=0, tiled=True)

    d_normed_two = scatter_all(times_transposed(d_gate_up, gate_own))
    gain_two = jnp.sum(d_normed_two * unit_two, axis=0)
    d_middle = upstream + norm_back(d_normed_two, unit_two, scale_two, ffn_gain, model_width)
    middle_b = d_middle.astype(BF16)
    middle_rows = gather_all(middle_b)
    block_out = middle + scatter_all(times(activated, down_own))

    def back_to_rows(part, width):
        pieces = [part[:, k * width : (k + 1) * width] for k in range(col_count)]
        got = [pieces[0]] + [
            swap(piece, "col", offset) for offset, piece in enumerate(pieces) if offset
        ]
        whole = lax.all_gather(jnp.concatenate(got, axis=1), "dp", axis=0, tiled=True)
        return [whole[:, k * width : (k + 1) * width] for k in range(col_count)]

    down_blocks = back_to_rows(down_part, local_width)
    gate_blocks = back_to_rows(gate_part, 2 * hidden_cols)
    grad_down = natural_cols(down_blocks, 0).astype(F32)
    grad_gate = natural_cols([block[:, :hidden_cols] for block in gate_blocks], 1).astype(F32)
    grad_up = natural_cols([block[:, hidden_cols:] for block in gate_blocks], 1).astype(F32)

    d_attn_f = times_transposed(middle_rows, out_own)
    out_terms = contract_rows(attn_cols, middle_rows[:, :local_width]).astype(BF16)
    d_attn = d_attn_f.astype(BF16).reshape(length, key_heads, group_size, head_width)
    d_qrot, d_krot, d_value = attention_backward(
        q_rot, k_rot, v_rows, segments, positions, log_totals, d_attn, attn_b, block_rows
    )
    dq_turn = rotate(d_qrot.reshape(length, key_heads * group_size, head_width), cosine, sine, -1.0)
    dk_turn = rotate(d_krot, cosine, sine, -1.0)
    query_gain_part = jnp.sum(dq_turn * q_unit, axis=(0, 1))
    key_gain_part = jnp.sum(dk_turn * k_unit, axis=(0, 1))
    d_query = head_norm_back(dq_turn, q_unit, q_scale, query_gain)
    d_key = head_norm_back(dk_turn, k_unit, k_scale, key_gain)
    d_qkv = jnp.concatenate(
        [
            d_query.reshape(length, query_cols),
            d_key.reshape(length, key_cols),
            d_value.reshape(length, value_cols),
        ],
        axis=1,
    ).astype(BF16)
    d_qkv_cols = col_gather(d_qkv, 1)
    qkv_terms = contract_rows(rows_one[:, :local_width], d_qkv_cols).astype(BF16)
    qkv_sum, out_sum = lax.psum((qkv_terms, out_terms), "dp")
    own_cols = query_cols + key_cols + value_cols
    qkv_blocks = [qkv_sum[:, k * own_cols : (k + 1) * own_cols] for k in range(col_count)]
    grad_query = natural_cols([b[:, :query_cols] for b in qkv_blocks], 1).astype(F32)
    grad_key = natural_cols(
        [b[:, query_cols : query_cols + key_cols] for b in qkv_blocks], 1
    ).astype(F32)
    grad_value = natural_cols([b[:, query_cols + key_cols :] for b in qkv_blocks], 1).astype(F32)
    grad_out = natural_cols(
        [out_sum[k * query_cols : (k + 1) * query_cols] for k in range(col_count)], 0
    ).astype(F32)

    d_normed_one = scatter_rows(times_transposed(d_qkv_cols, qkv_local))
    gain_one = jnp.sum(d_normed_one * unit_one, axis=0)
    in_grad = d_middle + norm_back(d_normed_one, unit_one, scale_one, attn_gain, model_width)

    gain_sums = all_total(
        jnp.concatenate([gain_one, gain_two, query_gain_part, key_gain_part]), ("row", "dp")
    )
    grad_attn_gain = gain_sums[:local_width]
    grad_ffn_gain = gain_sums[local_width : 2 * local_width]
    head_gains = all_total(gain_sums[2 * local_width :], ("col",))
    grad_query_gain = head_gains[:head_width]
    grad_key_gain = head_gains[head_width:]
    return (
        block_out[None],
        in_grad[None],
        grad_attn_gain,
        grad_query,
        grad_key,
        grad_value,
        grad_query_gain,
        grad_key_gain,
        grad_out,
        grad_ffn_gain,
        grad_gate,
        grad_up,
        grad_down,
    )


def solution(mesh):
    placed = (
        P("dp", "row", "col"),
        P("dp", "row", "col"),
        P("dp", None),
        P("col"),
        P("col", "row"),
        P("col", "row"),
        P("col", "row"),
        P(),
        P(),
        P("row", "col"),
        P("col"),
        P("col", "row"),
        P("col", "row"),
        P("row", "col"),
    )
    return jax.shard_map(
        body,
        mesh=mesh,
        in_specs=placed,
        out_specs=(
            P("dp", "row", "col"),
            P("dp", "row", "col"),
            P("col"),
            P("col", "row"),
            P("col", "row"),
            P("col", "row"),
            P(),
            P(),
            P("row", "col"),
            P("col"),
            P("col", "row"),
            P("col", "row"),
            P("row", "col"),
        ),
        check_vma=False,
    )
```

time: 816 us -> 444 us (0.54)
  waiting for transfers between devices: 566 us -> 208 us
  blocking collectives: 69.6 us -> 0 us
  starting transfers between devices: 1.3 us -> 45.5 us
  local copies, waits for them, and re-layouts: 41.5 us -> 72.7 us
  matrix products: 66.4 us -> 39.9 us
  other arithmetic: 46.4 us -> 56.3 us
    reduce_scatter x7 -> x2, waiting for transfers between devices: 206 us -> 5.29 us  [the longest x1 5.27 us: body(): lax.psum_scatter(gate_terms, 'dp', scatter_dimension=0, tiled=True)]
    ppermute x0 -> x51, waiting for transfers between devices: none -> 112 us  [swap(): return lax.ppermute(values, axis, [(i, i ^ bit) for i in range(count)])]
    all_gather x7 -> x2, waiting for transfers between devices: 165 us -> 56 us  [back_to_rows(): lax.all_gather(jnp.concatenate(got, axis=1), 'dp', axis=0, tiled=True)]
    psum x1, waiting for transfers between devices: 141 us -> 34.8 us  [body(): qkv_sum, out_sum = lax.psum((qkv_terms, out_terms), 'dp')]
    psum x5 -> x0, blocking collectives: 61 us -> none  [the longest x1 39.4 us: body(): lax.psum((padded_one, padded_two, query_gain_part, key_gain_part), ('dp',...]
    unnamed x17 -> x5, waiting for transfers between devices: 54.1 us -> 0.08 us
    ppermute x0 -> x51, starting transfers between devices: none -> 44.9 us  [swap(): return lax.ppermute(values, axis, [(i, i ^ bit) for i in range(count)])]
    concatenate x3 -> x27, other arithmetic: 6.29 us -> 23.6 us  [the longest x4 8.56 us: gather_all(): jnp.concatenate([one.reshape(-1, half, width), two.reshape(-1, half, widt...]
  transfers between devices with their start and end apart: 16 -> 56, of which waited for: 15 -> 33; matrix products, arithmetic and copies ran while one was open for 9% -> 28% of each run, Pallas kernels for 0% -> 0%
where the time goes in v1:
time: 444 us; the launch traced here: 439 us
  waiting for transfers between devices  208 us (47%)
  local copies, waits for them, and re-layouts  72.7 us (16%)
  other arithmetic  56.3 us (13%)
  starting transfers between devices  45.5 us (10%)
  matrix products  39.9 us (9%)
  between operations  16.2 us (4%)
    ppermute x51, waiting for transfers between devices, swap(): return lax.ppermute(values, axis, [(i, i ^ bit) for i in range(count)])  112 us
    all_gather x2, waiting for transfers between devices, back_to_rows(): lax.all_gather(jnp.concatenate(got, axis=1), 'dp', axis=0, tiled=True)  56 us
    ppermute x51, starting transfers between devices, swap(): return lax.ppermute(values, axis, [(i, i ^ bit) for i in range(count)])  44.9 us
    psum x1, waiting for transfers between devices, body(): qkv_sum, out_sum = lax.psum((qkv_terms, out_terms), 'dp')  34.8 us
    unnamed x258, local copies, waits for them, and re-layouts  32.7 us
    dot_general x5, matrix products, contract_rows(): lax.dot_general(left, right, (((0,), (0,)), ((), ())), preferred_element_...  9.94 us
    dot_general x4, matrix products, times_transposed(): lax.dot_general(left, right, (((1,), (1,)), ((), ())), preferred_element_...  9.28 us
  transfers between devices with their start and end apart: 56, of which 33 were waited for; matrix products, arithmetic and copies ran while one was open for 28% of the time, Pallas kernels for 0%

profile of v1, /device:TPU:0, one launch (start us, length us, event | category | flops | bytes accessed | tf_op | source)
XLA Modules:
  0.0 439.0 jit_solution(6110773348689635417)
XLA Ops:
  7.3 1.7 constant_dynamic-slice_fusion.25
  9.0 2.0 constant_dynamic-slice_fusion.23
  11.8 3.0 collective-permute-start.6
  15.1 6.2 %collective-permute-done = f32[256]{0:T(256)S(1)} collective-permute-done((f32[256]{0:T(256)S(1)}, f32[256]{0:T(256)S(1)}, u32[]{:S(2)}, u32[]{:S(2)}) %collective-permute-start) | collective-permute-done | bytes 1056 | tf_op jit(solution)/shard_map/ppermute | solution.py:37
  21.6 1.8 collective-permute-start.2
  26.6 1.8 collective-permute-done.1
  31.8 3.1 collective-permute-done.4
  42.4 1.8 fusion.74
  55.0 7.5 %collective-permute-done.7 = bf16[1024,128]{0,1:T(8,128)(2,1)S(1)} collective-permute-done((bf16[1024,128]{0,1:T(8,128)(2,1)S(1)}, bf16[1024,128]{0,1:T(8,128)(2,1)S(1)}, u32[]{:S(2)}, u32[]{:S(2)}) %collective-permute-start.7) | collective-permute-done | bytes 262176 | tf_op jit(solution)/shard_map/ppermute | solution.py:37
  72.0 1.6 collective-permute-start.24
  74.1 8.7 %collective-permute-done.24 = bf16[128,512]{0,1:T(8,128)(2,1)S(1)} collective-permute-done((bf16[128,512]{0,1:T(8,128)(2,1)S(1)}, bf16[128,512]{0,1:T(8,128)(2,1)S(1)}, u32[]{:S(2)}, u32[]{:S(2)}) %collective-permute-start.24) | collective-permute-done | bytes 131104 | tf_op jit(solution)/shard_map/ppermute | solution.py:37
  89.8 2.6 constant_dynamic-slice_fusion.2
  92.3 1.6 collective-permute-done.26
  100.0 2.0 reshape.456
  102.0 2.0 reshape.457
  104.0 2.8 pad_maximum_fusion.7
  108.0 1.8 pad_maximum_fusion.16
  109.8 2.0 reshape.452
  111.7 1.9 pad_maximum_fusion.17
  113.6 2.0 reshape.453
  115.6 2.4 pad_maximum_fusion.6
  119.1 1.7 collective-permute-start.16
  124.4 23.6 %collective-permute-done.16 = bf16[512,1152]{1,0:T(8,128)(2,1)S(1)} collective-permute-done((bf16[512,1152]{1,0:T(8,128)(2,1)S(1)}, bf16[512,1152]{1,0:T(8,128)(2,1)S(1)}, u32[]{:S(2)}, u32[]{:S(2)}) %collective-permute-start.16) | collective-permute-done | bytes 1179680 | tf_op jit(solution)/shard_map/ppermute | solution.py:37
  148.0 3.0 fusion.56
  151.1 8.7 %collective-permute-done.17 = bf16[576,512]{1,0:T(8,128)(2,1)S(1)} collective-permute-done((bf16[576,512]{1,0:T(8,128)(2,1)S(1)}, bf16[576,512]{1,0:T(8,128)(2,1)S(1)}, u32[]{:S(2)}, u32[]{:S(2)}) %collective-permute-start.17) | collective-permute-done | bytes 589856 | tf_op jit(solution)/shard_map/ppermute | solution.py:37
  159.7 2.9 multiply_convert_fusion.1
  162.7 3.1 fusion.54
  167.2 1.8 fusion.59
  169.0 2.0 copy-done.7
  172.7 2.7 convolution_convert_fusion.2
  175.5 2.2 slice_add_fusion
  180.1 1.8 copy.84
  181.9 1.7 collective-permute-start.29
  183.6 1.8 copy.85
  186.9 2.2 slice_add_fusion.1
  193.3 2.0 copy.86
  195.3 1.8 copy.80
  199.0 2.0 copy.82
  201.0 1.8 copy.81
  205.5 1.8 collective-permute-start.31
  208.8 3.0 collective-permute-done.20
  213.3 1.7 collective-permute-start.22
  221.2 2.2 collective-permute-start.34
  223.4 3.6 collective-permute-done.35
  227.8 2.1 collective-permute-start.37
  231.8 2.6 collective-permute-done.37
  234.3 2.0 collective-permute-done.36
  239.5 2.3 pad_maximum_fusion.8
  242.1 2.9 convolution_convert_fusion.1
  264.9 13.0 %collective-permute-done.40 = bf16[1024,256]{0,1:T(8,128)(2,1)S(1)} collective-permute-done((bf16[1024,256]{0,1:T(8,128)(2,1)S(1)}, bf16[1024,256]{0,1:T(8,128)(2,1)S(1)}, u32[]{:S(2)}, u32[]{:S(2)}) %collective-permute-start.40) | collective-permute-done | bytes 524320 | tf_op jit(solution)/shard_map/ppermute | solution.py:37
  282.1 1.8 fusion.94
  285.3 1.9 collective-permute-done.50
  290.4 5.3 %reduce-scatter.3.cloned.1.call-done = bf16[128,2304]{1,0:T(8,128)(2,1)} async-done(((bf16[512,2304]{1,0:T(8,128)(2,1)}), bf16[128,2304]{1,0:T(8,128)(2,1)}) %reduce-scatter.3.cloned.1.call-update) | async-done | bytes 589840 | tf_op jit(solution)/shard_map/reduce_scatter | solution.py:398
  300.4 4.9 %collective-permute-done.49 = bf16[128,1152]{1,0:T(8,128)(2,1)} collective-permute-done((bf16[128,1152]{1,0:T(8,128)(2,1)S(1)}, bf16[128,1152]{1,0:T(8,128)(2,1)}, u32[]{:S(2)}, u32[]{:S(2)}) %collective-permute-start.49) | collective-permute-done | bytes 294944 | tf_op jit(solution)/shard_map/ppermute | solution.py:37
  305.4 1.8 pad_maximum_fusion.12
  307.2 34.8 %all-reduce.3.cloned.1.call-done = (bf16[512,512]{1,0:T(8,128)(2,1)}, bf16[256,512]{1,0:T(8,128)(2,1)}) async-done(((bf16[512,512]{1,0:T(8,128)(2,1)}, bf16[256,512]{1,0:T(8,128)(2,1)}), (bf16[512,512]{1,0:T(8,128)(2,1)}, bf16[256,512]{1,0:T(8,128)(2,1)})) %all-reduce.3.cloned.1.call-update) | async-done | bytes 786448 | tf_op jit(solution)/shard_map/psum | solution.py:443
  352.3 3.4 collective-permute-done.46
  357.4 4.0 collective-permute-done.47
  365.6 8.6 %all-gather.5.cloned.1.call-done = bf16[576,1024]{1,0:T(8,128)(2,1)} async-done(((bf16[144,1024]{1,0:T(8,128)(2,1)}), bf16[576,1024]{1,0:T(8,128)(2,1)}) %all-gather.5.cloned.1.call-update) | async-done | bytes 1179664 | tf_op jit(solution)/shard_map/all_gather | solution.py:412
  375.9 1.7 maximum_convert_fusion.2
  377.6 47.5 %all-gather.3.cloned.1.call-done = bf16[512,2304]{1,0:T(8,128)(2,1)} async-done(((bf16[128,2304]{1,0:T(8,128)(2,1)}), bf16[512,2304]{1,0:T(8,128)(2,1)}) %all-gather.3.cloned.1.call-update) | async-done | bytes 2359312 | tf_op jit(solution)/shard_map/all_gather | solution.py:412
  425.1 2.4 slice_bitcast_fusion
  428.1 1.8 maximum_convert_fusion.1
  430.4 1.8 maximum_convert_fusion
  (506 shorter events, 137.2 us)
Async XLA Ops:
  7.2 273.5 %reduce-scatter.5.cloned.1.call-start = ((), (), s32[]{:S(2)}) async-start(), calls=%async_computation.4 | async-start | bytes 1474560 | tf_op jit(solution)/shard_map/reduce_scatter | solution.py:397
  9.0 15.9 %copy-start.106 = (s32[1,1024]{1,0:T(1,128)S(1)}, s32[1,1024]{1,0:T(1,128)}, u32[]{:S(2)}) copy-start(s32[1,1024]{1,0:T(1,128)} %param.16) | copy-start | bytes 12292
  10.9 30.5 %copy-start.63 = (bf16[512,64]{1,0:T(8,128)(2,1)}, bf16[512,64]{1,0:T(8,128)(2,1)S(1)}, u32[]{:S(2)}) copy-start(bf16[512,64]{1,0:T(8,128)(2,1)S(1)} %get-tuple-element.175) | copy-start | bytes 196612
  11.8 29.7 %collective-permute-start.6 = (bf16[512,256]{1,0:T(8,128)(2,1)}, bf16[512,256]{1,0:T(8,128)(2,1)}, u32[]{:S(2)}, u32[]{:S(2)}) collective-permute-start(bf16[512,256]{1,0:T(8,128)(2,1)} %pad_maximum_fusion.31), channel_id=1, source_target_pairs={{0,1},{1,0},{2,3},{3,2},{4,5},{5,4},{6,7},{7,6},{8,9},{9,8},{10,11... | collective-permute-start | bytes 786440 | tf_op jit(solution)/shard_map/ppermute | solution.py:37
  15.0 6.3 %collective-permute-start = (f32[256]{0:T(256)S(1)}, f32[256]{0:T(256)S(1)}, u32[]{:S(2)}, u32[]{:S(2)}) collective-permute-start(f32[256]{0:T(256)S(1)} %fusion.86), channel_id=1, source_target_pairs={{0,1},{1,0},{2,3},{3,2},{4,5},{5,4},{6,7},{7,6},{8,9},{9,8},{10,11... | collective-permute-start | bytes 3080 | tf_op jit(solution)/shard_map/ppermute | solution.py:37
  21.6 5.0 %collective-permute-start.2 = (bf16[128,512]{0,1:T(8,128)(2,1)S(1)}, bf16[128,512]{0,1:T(8,128)(2,1)S(1)}, u32[]{:S(2)}, u32[]{:S(2)}) collective-permute-start(bf16[128,512]{0,1:T(8,128)(2,1)S(1)} %get-tuple-element.159), channel_id=1, source_target_pairs={{0,4},{2,6},{4,0},{6,2},{1,5},{3,7},{5,1},{7,3},{8,12},{10,14},{12... | collective-permute-start | bytes 393224 | tf_op jit(solution)/shard_map/ppermute | solution.py:37
  23.4 5.0 %collective-permute-start.1 = (bf16[128,512]{0,1:T(8,128)(2,1)S(1)}, bf16[128,512]{0,1:T(8,128)(2,1)S(1)}, u32[]{:S(2)}, u32[]{:S(2)}) collective-permute-start(bf16[128,512]{0,1:T(8,128)(2,1)S(1)} %get-tuple-element.160), channel_id=1, source_target_pairs={{0,1},{1,0},{2,3},{3,2},{4,5},{5,4},{6,7},{7,6},{8,9},{9,8},{10,11... | collective-permute-start | bytes 393224 | tf_op jit(solution)/shard_map/ppermute | solution.py:37
  28.4 6.4 %collective-permute-start.4 = (bf16[256,512]{0,1:T(8,128)(2,1)S(1)}, bf16[256,512]{0,1:T(8,128)(2,1)S(1)}, u32[]{:S(2)}, u32[]{:S(2)}) collective-permute-start(bf16[256,512]{0,1:T(8,128)(2,1)S(1)} %pad_maximum_fusion.30), channel_id=1, source_target_pairs={{0,1},{1,0},{2,3},{3,2},{4,5},{5,4},{6,7},{7,6},{8,9},{9,8},{10,11... | collective-permute-start | bytes 786440 | tf_op jit(solution)/shard_map/ppermute | solution.py:37
  30.0 6.4 %collective-permute-start.3 = (bf16[128,1024]{0,1:T(8,128)(2,1)S(1)}, bf16[128,1024]{0,1:T(8,128)(2,1)S(1)}, u32[]{:S(2)}, u32[]{:S(2)}) collective-permute-start(bf16[128,1024]{0,1:T(8,128)(2,1)S(1)} %pad_maximum_fusion.29), channel_id=1, source_target_pairs={{0,4},{2,6},{4,0},{6,2},{1,5},{3,7},{5,1},{7,3},{8,12},{10,14},{12... | collective-permute-start | bytes 786440 | tf_op jit(solution)/shard_map/ppermute | solution.py:37
  38.2 3.1 collective-permute-start.5
  53.7 8.8 %collective-permute-start.7 = (bf16[1024,128]{0,1:T(8,128)(2,1)S(1)}, bf16[1024,128]{0,1:T(8,128)(2,1)S(1)}, u32[]{:S(2)}, u32[]{:S(2)}) collective-permute-start(bf16[1024,128]{0,1:T(8,128)(2,1)S(1)} %pad_maximum_fusion.32), channel_id=1, source_target_pairs={{0,1},{1,0},{2,3},{3,2},{4,5},{5,4},{6,7},{7,6},{8,9},{9,8},{10,11... | collective-permute-start | bytes 786440 | tf_op jit(solution)/shard_map/ppermute | solution.py:37
  66.2 2.1 collective-permute-start.8
  70.7 17.6 %copy-start.89 = (f32[512]{0:T(512)S(1)}, f32[512]{0:T(512)}, u32[]{:S(2)}) copy-start(f32[512]{0:T(512)} %param.24) | copy-start | bytes 6148
  71.4 12.1 %collective-permute-start.9 = (bf16[256,512]{0,1:T(8,128)(2,1)}, bf16[256,512]{0,1:T(8,128)(2,1)S(1)}, u32[]{:S(2)}, u32[]{:S(2)}) collective-permute-start(bf16[256,512]{0,1:T(8,128)(2,1)} %slice.607), channel_id=1, source_target_pairs={{0,4},{2,6},{4,0},{6,2},{1,5},{3,7},{5,1},{7,3},{8,12},{10,14},{12... | collective-permute-start | bytes 786440 | tf_op jit(solution)/shard_map/ppermute | solution.py:37
  72.0 16.5 %copy-start.48 = (bf16[128,512]{0,1:T(8,128)(2,1)}, bf16[128,512]{0,1:T(8,128)(2,1)S(1)}, u32[]{:S(2)}) copy-start(bf16[128,512]{0,1:T(8,128)(2,1)S(1)} %get-tuple-element.153) | copy-start | bytes 393220
  72.0 10.8 %collective-permute-start.24 = (bf16[128,512]{0,1:T(8,128)(2,1)S(1)}, bf16[128,512]{0,1:T(8,128)(2,1)S(1)}, u32[]{:S(2)}, u32[]{:S(2)}) collective-permute-start(bf16[128,512]{0,1:T(8,128)(2,1)S(1)} %get-tuple-element.153), channel_id=1, source_target_pairs={{0,4},{2,6},{4,0},{6,2},{1,5},{3,7},{5,1},{7,3},{8,12},{10,14},{12... | collective-permute-start | bytes 393224 | tf_op jit(solution)/shard_map/ppermute | solution.py:37
  73.5 9.2 %collective-permute-start.23 = (bf16[128,512]{0,1:T(8,128)(2,1)S(1)}, bf16[128,512]{0,1:T(8,128)(2,1)S(1)}, u32[]{:S(2)}, u32[]{:S(2)}) collective-permute-start(bf16[128,512]{0,1:T(8,128)(2,1)S(1)} %get-tuple-element.154), channel_id=1, source_target_pairs={{0,1},{1,0},{2,3},{3,2},{4,5},{5,4},{6,7},{7,6},{8,9},{9,8},{10,11... | collective-permute-start | bytes 393224 | tf_op jit(solution)/shard_map/ppermute | solution.py:37
  74.1 15.7 %copy-start.16 = (bf16[512,1152]{1,0:T(8,128)(2,1)S(1)}, bf16[512,1152]{1,0:T(8,128)(2,1)}, u32[]{:S(2)}) copy-start(bf16[512,1152]{1,0:T(8,128)(2,1)} %param.25) | copy-start | bytes 3538948
  84.6 3.6 collective-permute-start.10
  85.3 8.7 %collective-permute-start.26 = (bf16[256,512]{0,1:T(8,128)(2,1)S(1)}, bf16[256,512]{0,1:T(8,128)(2,1)S(1)}, u32[]{:S(2)}, u32[]{:S(2)}) collective-permute-start(bf16[256,512]{0,1:T(8,128)(2,1)S(1)} %pad_maximum_fusion.36), channel_id=1, source_target_pairs={{0,1},{1,0},{2,3},{3,2},{4,5},{5,4},{6,7},{7,6},{8,9},{9,8},{10,11... | collective-permute-start | bytes 786440 | tf_op jit(solution)/shard_map/ppermute | solution.py:37
  86.8 8.3 %collective-permute-start.25 = (bf16[128,1024]{0,1:T(8,128)(2,1)S(1)}, bf16[128,1024]{0,1:T(8,128)(2,1)S(1)}, u32[]{:S(2)}, u32[]{:S(2)}) collective-permute-start(bf16[128,1024]{0,1:T(8,128)(2,1)S(1)} %pad_maximum_fusion.35), channel_id=1, source_target_pairs={{0,4},{2,6},{4,0},{6,2},{1,5},{3,7},{5,1},{7,3},{8,12},{10,14},{12... | collective-permute-start | bytes 786440 | tf_op jit(solution)/shard_map/ppermute | solution.py:37
  88.5 8.1 %collective-permute-start.12 = (bf16[128,512]{0,1:T(8,128)(2,1)S(1)}, bf16[128,512]{0,1:T(8,128)(2,1)S(1)}, u32[]{:S(2)}, u32[]{:S(2)}) collective-permute-start(bf16[128,512]{0,1:T(8,128)(2,1)S(1)} %get-tuple-element.155), channel_id=1, source_target_pairs={{0,4},{2,6},{4,0},{6,2},{1,5},{3,7},{5,1},{7,3},{8,12},{10,14},{12... | collective-permute-start | bytes 393224 | tf_op jit(solution)/shard_map/ppermute | solution.py:37
  89.2 7.4 %collective-permute-start.11 = (bf16[128,512]{0,1:T(8,128)(2,1)S(1)}, bf16[128,512]{0,1:T(8,128)(2,1)S(1)}, u32[]{:S(2)}, u32[]{:S(2)}) collective-permute-start(bf16[128,512]{0,1:T(8,128)(2,1)S(1)} %get-tuple-element.156), channel_id=1, source_target_pairs={{0,1},{1,0},{2,3},{3,2},{4,5},{5,4},{6,7},{7,6},{8,9},{9,8},{10,11... | collective-permute-start | bytes 393224 | tf_op jit(solution)/shard_map/ppermute | solution.py:37
  98.1 9.9 %collective-permute-start.14 = (bf16[256,512]{0,1:T(8,128)(2,1)}, bf16[256,512]{0,1:T(8,128)(2,1)}, u32[]{:S(2)}, u32[]{:S(2)}) collective-permute-start(bf16[256,512]{0,1:T(8,128)(2,1)} %pad_maximum_fusion.34), channel_id=1, source_target_pairs={{0,1},{1,0},{2,3},{3,2},{4,5},{5,4},{6,7},{7,6},{8,9},{9,8},{10,11... | collective-permute-start | bytes 786440 | tf_op jit(solution)/shard_map/ppermute | solution.py:37
  98.6 9.3 %collective-permute-start.13 = (bf16[128,1024]{0,1:T(8,128)(2,1)}, bf16[128,1024]{0,1:T(8,128)(2,1)}, u32[]{:S(2)}, u32[]{:S(2)}) collective-permute-start(bf16[128,1024]{0,1:T(8,128)(2,1)} %pad_maximum_fusion.33), channel_id=1, source_target_pairs={{0,4},{2,6},{4,0},{6,2},{1,5},{3,7},{5,1},{7,3},{8,12},{10,14},{12... | collective-permute-start | bytes 786440 | tf_op jit(solution)/shard_map/ppermute | solution.py:37
  107.9 14.8 %collective-permute-start.27 = (bf16[512,1024]{0,1:T(8,128)(2,1)}, bf16[512,1024]{0,1:T(8,128)(2,1)}, u32[]{:S(2)}, u32[]{:S(2)}) collective-permute-start(bf16[512,1024]{0,1:T(8,128)(2,1)} %bitcast.137), channel_id=1, source_target_pairs={{0,2},{2,0},{4,6},{6,4},{1,3},{3,1},{5,7},{7,5},{8,10},{10,8},{12,... | collective-permute-start | bytes 3145736 | tf_op jit(solution)/shard_map/ppermute | solution.py:37
  118.2 6.0 %collective-permute-start.15 = (bf16[512,1024]{0,1:T(8,128)(2,1)S(1)}, bf16[512,1024]{0,1:T(8,128)(2,1)S(1)}, u32[]{:S(2)}, u32[]{:S(2)}) collective-permute-start(bf16[512,1024]{0,1:T(8,128)(2,1)S(1)} %bitcast.391), channel_id=1, source_target_pairs={{0,2},{2,0},{4,6},{6,4},{1,3},{3,1},{5,7},{7,5},{8,10},{10,8},{12,... | collective-permute-start | bytes 3145736 | tf_op jit(solution)/shard_map/ppermute | solution.py:37
  119.1 28.9 %collective-permute-start.16 = (bf16[512,1152]{1,0:T(8,128)(2,1)S(1)}, bf16[512,1152]{1,0:T(8,128)(2,1)S(1)}, u32[]{:S(2)}, u32[]{:S(2)}) collective-permute-start(bf16[512,1152]{1,0:T(8,128)(2,1)S(1)} %pad_maximum_fusion.3), channel_id=1, source_target_pairs={{0,1},{1,0},{2,3},{3,2},{4,5},{5,4},{6,7},{7,6},{8,9},{9,8},{10,11... | collective-permute-start | bytes 3538952 | tf_op jit(solution)/shard_map/ppermute | solution.py:37
  121.0 38.8 %collective-permute-start.17 = (bf16[576,512]{1,0:T(8,128)(2,1)S(1)}, bf16[576,512]{1,0:T(8,128)(2,1)S(1)}, u32[]{:S(2)}, u32[]{:S(2)}) collective-permute-start(bf16[576,512]{1,0:T(8,128)(2,1)S(1)} %get-tuple-element.117), channel_id=1, source_target_pairs={{0,1},{1,0},{2,3},{3,2},{4,5},{5,4},{6,7},{7,6},{8,9},{9,8},{10,11... | collective-permute-start | bytes 1769480 | tf_op jit(solution)/shard_map/ppermute | solution.py:37
  124.1 24.0 %copy-start.57 = (bf16[512,576]{1,0:T(8,128)(2,1)S(1)}, bf16[512,576]{1,0:T(8,128)(2,1)}, u32[]{:S(2)}) copy-start(bf16[512,576]{1,0:T(8,128)(2,1)} %get-tuple-element.121) | copy-start | bytes 1769476
  124.1 23.9 %copy-start.58 = (bf16[512,576]{1,0:T(8,128)(2,1)S(1)}, bf16[512,576]{1,0:T(8,128)(2,1)}, u32[]{:S(2)}) copy-start(bf16[512,576]{1,0:T(8,128)(2,1)} %get-tuple-element.209) | copy-start | bytes 1769476
  124.4 26.7 %copy-start.70 = (bf16[1024,1024]{0,1:T(8,128)(2,1)}, bf16[1024,1024]{0,1:T(8,128)(2,1)S(1)}, u32[]{:S(2)}) copy-start(bf16[1024,1024]{0,1:T(8,128)(2,1)S(1)} %constant_dynamic-update-slice_fusion.2) | copy-start | bytes 6291460
  167.2 8.3 %collective-permute-start.28 = (bf16[512,1024]{1,0:T(8,128)(2,1)}, bf16[512,1024]{1,0:T(8,128)(2,1)}, u32[]{:S(2)}, u32[]{:S(2)}) collective-permute-start(bf16[512,1024]{1,0:T(8,128)(2,1)} %slice.602), channel_id=1, source_target_pairs={{0,2},{2,0},{4,6},{6,4},{1,3},{3,1},{5,7},{7,5},{8,10},{10,8},{12,... | collective-permute-start | bytes 3145736 | tf_op jit(solution)/shard_map/ppermute | solution.py:37
  172.2 14.7 %collective-permute-start.18 = (bf16[512,1024]{1,0:T(8,128)(2,1)}, bf16[512,1024]{1,0:T(8,128)(2,1)}, u32[]{:S(2)}, u32[]{:S(2)}) collective-permute-start(bf16[512,1024]{1,0:T(8,128)(2,1)} %slice.603), channel_id=1, source_target_pairs={{0,2},{2,0},{4,6},{6,4},{1,3},{3,1},{5,7},{7,5},{8,10},{10,8},{12,... | collective-permute-start | bytes 3145736 | tf_op jit(solution)/shard_map/ppermute | solution.py:37
  175.5 120.3 %reduce-scatter.3.cloned.1.call-start = ((), (), s32[]{:S(2)}) async-start(), calls=%async_computation.2 | async-start | bytes 2949120 | tf_op jit(solution)/shard_map/reduce_scatter | solution.py:398
  181.9 21.2 %collective-permute-start.29 = (bf16[128,1024]{0,1:T(8,128)(2,1)}, bf16[128,1024]{0,1:T(8,128)(2,1)}, u32[]{:S(2)}, u32[]{:S(2)}) collective-permute-start(bf16[128,1024]{0,1:T(8,128)(2,1)} %bitcast.420), channel_id=1, source_target_pairs={{0,4},{2,6},{4,0},{6,2},{1,5},{3,7},{5,1},{7,3},{8,12},{10,14},{12... | collective-permute-start | bytes 786440 | tf_op jit(solution)/shard_map/ppermute | solution.py:37
  185.4 17.8 %collective-permute-start.30 = (bf16[256,512]{0,1:T(8,128)(2,1)}, bf16[256,512]{0,1:T(8,128)(2,1)}, u32[]{:S(2)}, u32[]{:S(2)}) collective-permute-start(bf16[256,512]{0,1:T(8,128)(2,1)} %copy.85), channel_id=1, source_target_pairs={{0,1},{1,0},{2,3},{3,2},{4,5},{5,4},{6,7},{7,6},{8,9},{9,8},{10,11... | collective-permute-start | bytes 786440 | tf_op jit(solution)/shard_map/ppermute | solution.py:37
  197.2 11.6 %collective-permute-start.19 = (bf16[128,1024]{0,1:T(8,128)(2,1)}, bf16[128,1024]{0,1:T(8,128)(2,1)}, u32[]{:S(2)}, u32[]{:S(2)}) collective-permute-start(bf16[128,1024]{0,1:T(8,128)(2,1)} %bitcast.360), channel_id=1, source_target_pairs={{0,4},{2,6},{4,0},{6,2},{1,5},{3,7},{5,1},{7,3},{8,12},{10,14},{12... | collective-permute-start | bytes 786440 | tf_op jit(solution)/shard_map/ppermute | solution.py:37
  202.8 9.0 %collective-permute-start.20 = (bf16[256,512]{0,1:T(8,128)(2,1)}, bf16[256,512]{0,1:T(8,128)(2,1)S(1)}, u32[]{:S(2)}, u32[]{:S(2)}) collective-permute-start(bf16[256,512]{0,1:T(8,128)(2,1)} %copy.81), channel_id=1, source_target_pairs={{0,1},{1,0},{2,3},{3,2},{4,5},{5,4},{6,7},{7,6},{8,9},{9,8},{10,11... | collective-permute-start | bytes 786440 | tf_op jit(solution)/shard_map/ppermute | solution.py:37
  205.5 9.5 %collective-permute-start.31 = (bf16[128,512]{0,1:T(8,128)(2,1)S(1)}, bf16[128,512]{0,1:T(8,128)(2,1)S(1)}, u32[]{:S(2)}, u32[]{:S(2)}) collective-permute-start(bf16[128,512]{0,1:T(8,128)(2,1)S(1)} %slice.609), channel_id=1, source_target_pairs={{0,1},{1,0},{2,3},{3,2},{4,5},{5,4},{6,7},{7,6},{8,9},{9,8},{10,11... | collective-permute-start | bytes 393224 | tf_op jit(solution)/shard_map/ppermute | solution.py:37
  207.3 7.7 %collective-permute-start.32 = (bf16[128,512]{0,1:T(8,128)(2,1)S(1)}, bf16[128,512]{0,1:T(8,128)(2,1)S(1)}, u32[]{:S(2)}, u32[]{:S(2)}) collective-permute-start(bf16[128,512]{0,1:T(8,128)(2,1)S(1)} %slice.608), channel_id=1, source_target_pairs={{0,4},{2,6},{4,0},{6,2},{1,5},{3,7},{5,1},{7,3},{8,12},{10,14},{12... | collective-permute-start | bytes 393224 | tf_op jit(solution)/shard_map/ppermute | solution.py:37
  212.9 5.0 %collective-permute-start.21 = (bf16[128,512]{0,1:T(8,128)(2,1)S(1)}, bf16[128,512]{0,1:T(8,128)(2,1)S(1)}, u32[]{:S(2)}, u32[]{:S(2)}) collective-permute-start(bf16[128,512]{0,1:T(8,128)(2,1)S(1)} %slice.611), channel_id=1, source_target_pairs={{0,1},{1,0},{2,3},{3,2},{4,5},{5,4},{6,7},{7,6},{8,9},{9,8},{10,11... | collective-permute-start | bytes 393224 | tf_op jit(solution)/shard_map/ppermute | solution.py:37
  213.3 5.0 %collective-permute-start.22 = (bf16[128,512]{0,1:T(8,128)(2,1)S(1)}, bf16[128,512]{0,1:T(8,128)(2,1)S(1)}, u32[]{:S(2)}, u32[]{:S(2)}) collective-permute-start(bf16[128,512]{0,1:T(8,128)(2,1)S(1)} %slice.610), channel_id=1, source_target_pairs={{0,4},{2,6},{4,0},{6,2},{1,5},{3,7},{5,1},{7,3},{8,12},{10,14},{12... | collective-permute-start | bytes 393224 | tf_op jit(solution)/shard_map/ppermute | solution.py:37
  216.0 3.6 collective-permute-start.33
  220.6 6.4 %collective-permute-start.35 = (bf16[128,512]{0,1:T(8,128)(2,1)S(1)}, bf16[128,512]{0,1:T(8,128)(2,1)S(1)}, u32[]{:S(2)}, u32[]{:S(2)}) collective-permute-start(bf16[128,512]{0,1:T(8,128)(2,1)S(1)} %get-tuple-element.151), channel_id=1, source_target_pairs={{0,4},{2,6},{4,0},{6,2},{1,5},{3,7},{5,1},{7,3},{8,12},{10,14},{12... | collective-permute-start | bytes 393224 | tf_op jit(solution)/shard_map/ppermute | solution.py:37
  221.2 6.6 %collective-permute-start.34 = (bf16[128,512]{0,1:T(8,128)(2,1)S(1)}, bf16[128,512]{0,1:T(8,128)(2,1)S(1)}, u32[]{:S(2)}, u32[]{:S(2)}) collective-permute-start(bf16[128,512]{0,1:T(8,128)(2,1)S(1)} %get-tuple-element.152), channel_id=1, source_target_pairs={{0,1},{1,0},{2,3},{3,2},{4,5},{5,4},{6,7},{7,6},{8,9},{9,8},{10,11... | collective-permute-start | bytes 393224 | tf_op jit(solution)/shard_map/ppermute | solution.py:37
  227.8 6.5 %collective-permute-start.37 = (bf16[256,512]{0,1:T(8,128)(2,1)S(1)}, bf16[256,512]{0,1:T(8,128)(2,1)}, u32[]{:S(2)}, u32[]{:S(2)}) collective-permute-start(bf16[256,512]{0,1:T(8,128)(2,1)S(1)} %pad_maximum_fusion.38), channel_id=1, source_target_pairs={{0,1},{1,0},{2,3},{3,2},{4,5},{5,4},{6,7},{7,6},{8,9},{9,8},{10,11... | collective-permute-start | bytes 786440 | tf_op jit(solution)/shard_map/ppermute | solution.py:37
  229.9 6.5 %collective-permute-start.36 = (bf16[128,1024]{0,1:T(8,128)(2,1)S(1)}, bf16[128,1024]{0,1:T(8,128)(2,1)}, u32[]{:S(2)}, u32[]{:S(2)}) collective-permute-start(bf16[128,1024]{0,1:T(8,128)(2,1)S(1)} %pad_maximum_fusion.37), channel_id=1, source_target_pairs={{0,4},{2,6},{4,0},{6,2},{1,5},{3,7},{5,1},{7,3},{8,12},{10,14},{12... | collective-permute-start | bytes 786440 | tf_op jit(solution)/shard_map/ppermute | solution.py:37
  230.6 19.5 %collective-permute-start.39 = (bf16[128,512]{1,0:T(8,128)(2,1)}, bf16[128,512]{1,0:T(8,128)(2,1)}, u32[]{:S(2)}, u32[]{:S(2)}) collective-permute-start(bf16[128,512]{1,0:T(8,128)(2,1)} %get-tuple-element.162), channel_id=1, source_target_pairs={{0,1},{1,0},{2,3},{3,2},{4,5},{5,4},{6,7},{7,6},{8,9},{9,8},{10,11... | collective-permute-start | bytes 393224 | tf_op jit(solution)/shard_map/ppermute | solution.py:37
  242.0 6.6 %collective-permute-start.38 = (bf16[512,1024]{0,1:T(8,128)(2,1)S(1)}, bf16[512,1024]{0,1:T(8,128)(2,1)}, u32[]{:S(2)}, u32[]{:S(2)}) collective-permute-start(bf16[512,1024]{0,1:T(8,128)(2,1)S(1)} %bitcast.393), channel_id=1, source_target_pairs={{0,2},{2,0},{4,6},{6,4},{1,3},{3,1},{5,7},{7,5},{8,10},{10,8},{12,... | collective-permute-start | bytes 3145736 | tf_op jit(solution)/shard_map/ppermute | solution.py:37
  248.2 93.8 %all-reduce.3.cloned.1.call-start = ((), (), s32[]{:S(2)}) async-start(), calls=%async_computation.6 | async-start | bytes 1572864 | tf_op jit(solution)/shard_map/psum | solution.py:443
  263.6 14.3 %collective-permute-start.40 = (bf16[1024,256]{0,1:T(8,128)(2,1)S(1)}, bf16[1024,256]{0,1:T(8,128)(2,1)S(1)}, u32[]{:S(2)}, u32[]{:S(2)}) collective-permute-start(bf16[1024,256]{0,1:T(8,128)(2,1)S(1)} %pad_maximum_fusion.24), channel_id=1, source_target_pairs={{0,1},{1,0},{2,3},{3,2},{4,5},{5,4},{6,7},{7,6},{8,9},{9,8},{10,11... | collective-permute-start | bytes 1572872 | tf_op jit(solution)/shard_map/ppermute | solution.py:37
  280.3 93.9 %all-gather.5.cloned.1.call-start = ((), (), s32[]{:S(2)}) async-start(), calls=%async_computation.5 | async-start | bytes 1474560 | tf_op jit(solution)/shard_map/all_gather | solution.py:412
  281.7 5.5 %collective-permute-start.50 = (bf16[144,512]{1,0:T(8,128)(2,1)S(1)}, bf16[144,512]{1,0:T(8,128)(2,1)S(1)}, u32[]{:S(2)}, u32[]{:S(2)}) collective-permute-start(bf16[144,512]{1,0:T(8,128)(2,1)S(1)} %get-tuple-element.138), channel_id=1, source_target_pairs={{0,1},{1,0},{2,3},{3,2},{4,5},{5,4},{6,7},{7,6},{8,9},{9,8},{10,11... | collective-permute-start | bytes 442376 | tf_op jit(solution)/shard_map/ppermute | solution.py:37
  285.3 3.1 collective-permute-start.41
  288.0 137.1 %all-gather.3.cloned.1.call-start = ((), (), s32[]{:S(2)}) async-start(), calls=%async_computation.3 | async-start | bytes 2949120 | tf_op jit(solution)/shard_map/all_gather | solution.py:412
  289.8 9.7 %collective-permute-start.42 = (bf16[256,512]{0,1:T(8,128)(2,1)S(1)}, bf16[256,512]{0,1:T(8,128)(2,1)S(1)}, u32[]{:S(2)}, u32[]{:S(2)}) collective-permute-start(bf16[256,512]{0,1:T(8,128)(2,1)S(1)} %slice.606), channel_id=1, source_target_pairs={{0,4},{2,6},{4,0},{6,2},{1,5},{3,7},{5,1},{7,3},{8,12},{10,14},{12... | collective-permute-start | bytes 786440 | tf_op jit(solution)/shard_map/ppermute | solution.py:37
  296.8 8.5 %collective-permute-start.49 = (bf16[128,1152]{1,0:T(8,128)(2,1)S(1)}, bf16[128,1152]{1,0:T(8,128)(2,1)}, u32[]{:S(2)}, u32[]{:S(2)}) collective-permute-start(bf16[128,1152]{1,0:T(8,128)(2,1)S(1)} %get-tuple-element.127), channel_id=1, source_target_pairs={{0,1},{1,0},{2,3},{3,2},{4,5},{5,4},{6,7},{7,6},{8,9},{9,8},{10,11... | collective-permute-start | bytes 884744 | tf_op jit(solution)/shard_map/ppermute | solution.py:37
  299.7 52.6 %collective-permute-start.43 = (f32[256]{0:T(256)S(1)}, f32[256]{0:T(256)S(1)}, u32[]{:S(2)}, u32[]{:S(2)}) collective-permute-start(f32[256]{0:T(256)S(1)} %get-tuple-element.88), channel_id=1, source_target_pairs={{0,1},{1,0},{2,3},{3,2},{4,5},{5,4},{6,7},{7,6},{8,9},{9,8},{10,11... | collective-permute-start | bytes 3080 | tf_op jit(solution)/shard_map/ppermute | solution.py:37
  300.4 47.0 %collective-permute-start.44 = (f32[1152]{0:T(1024)S(1)}, f32[1152]{0:T(1024)S(1)}, u32[]{:S(2)}, u32[]{:S(2)}) collective-permute-start(f32[1152]{0:T(1024)S(1)} %concatenate.323), channel_id=1, source_target_pairs={{0,2},{2,0},{4,6},{6,4},{1,3},{3,1},{5,7},{7,5},{8,10},{10,8},{12,... | collective-permute-start | bytes 13832 | tf_op jit(solution)/shard_map/ppermute | solution.py:37
  347.4 3.7 collective-permute-start.45
  351.2 4.6 %collective-permute-start.46 = (f32[1152]{0:T(1024)S(1)}, f32[1152]{0:T(1024)S(1)}, u32[]{:S(2)}, u32[]{:S(2)}) collective-permute-start(f32[1152]{0:T(1024)S(1)} %add.296), channel_id=1, source_target_pairs={{0,8},{8,0},{16,24},{24,16},{1,9},{9,1},{17,25},{25,17},{2,10},{10... | collective-permute-start | bytes 13832 | tf_op jit(solution)/shard_map/ppermute | solution.py:37
  355.7 5.6 %collective-permute-start.47 = (f32[1152]{0:T(1024)S(1)}, f32[1152]{0:T(1024)S(1)}, u32[]{:S(2)}, u32[]{:S(2)}) collective-permute-start(f32[1152]{0:T(1024)S(1)} %add.297), channel_id=1, source_target_pairs={{0,16},{8,24},{16,0},{24,8},{1,17},{9,25},{17,1},{25,9},{2,18},{10... | collective-permute-start | bytes 13832 | tf_op jit(solution)/shard_map/ppermute | solution.py:37
  361.4 3.6 collective-permute-start.48
  (111 other events, 561.9 us)
Sparse Core Ops, SparseCore 0:
  175.6 30.7 reduce-scatter.4
  248.3 47.3 reduce-scatter.2
  298.7 43.2 all-reduce.2
  344.0 30.0 all-gather.4
  376.1 48.9 all-gather.2
